TPU v7x, 32 devices: a whole 2x2x4 slice. The times are simulated.
32 devices in a mesh: feat: 4 (over y, x), dom: 8 (over z, core).
Axes of the slice: x: 2, y: 2, z: 4, core: 2. Of those that a mesh axis runs over, the one named last changes fastest.
Arguments:
- features: bfloat16 [4, 8, 512, 1024], P(None, 'dom', None, 'feat'), may hold values from -100 to 100
- w_self: bfloat16 [1024, 256], P('feat'), may hold values from -0.1875 to 0.1875
- w_neigh: bfloat16 [1024, 256], P('feat'), may hold values from -2 to 2
- gain: float32 [256], replicated, may hold values from 0.5 to 1.5
- shift: float32 [256], replicated, may hold values from -1 to 1
- d_hidden: bfloat16 [4, 8, 512, 256], P('feat', 'dom'), may hold values from -32 to 32
- send_rows: int32 [4, 8, 32, 32], P('feat', 'dom'), may hold values from 0 to 511
- send_count: int32 [4, 8, 32], P('feat', 'dom'), may hold values from 0 to 32, as said below
- tile_src: int32 [4, 8, 136], P('feat', 'dom'), may hold values from 0 to 11, as said below
- tile_dst: int32 [4, 8, 136], P('feat', 'dom'), may hold values from 0 to 3
- tile_count: int32 [4, 8], P('feat', 'dom'), may hold values from 12 to 136, as said below
- tile_vals: bfloat16 [4, 8, 136, 128, 128], P('feat', 'dom'), may hold values from 0 to 1, as said below
Outputs:
- hidden: bfloat16 [4, 8, 512, 256], P('feat', 'dom')
- d_self: bfloat16 [4, 8, 512, 256], P('feat', 'dom')
- d_neigh: bfloat16 [4, 8, 512, 256], P('feat', 'dom')
- gain_grad: float32 [256], replicated
- shift_grad: float32 [256], replicated
Inputs may be any that keep to these rules, and one draw needn't show every extreme that they name: `send_rows`: rows may repeat within a list. `send_count`: the live slots are the first ones; in every draw some receiving partition gets 32 live slots from every partition. `tile_src`: blocks below 4 are the partition's own nodes, the others the halo rows in order of sender and slot; the first 12 tiles of each partition name every source block once. `tile_count`: the live tiles are the first ones; some partition has all 136 live. `tile_vals`: nonnegative; tiles past a partition's count are not used.
All inputs are finite; a program needn't handle non-finite values.
Results may differ from a plain program's by a relative error of at most 0.0056.
Values may be sent and summed in bfloat16 or wider, within the bound.
A program may use at most 64 MiB of HBM per device.

v0:
```python
import jax
import jax.numpy as jnp
from jax import lax
from jax.sharding import PartitionSpec as P

per_turn = 4
epsilon = 1e-05


def boundary_forward(outgoing):
    parts_total, slot_count, width = outgoing.shape
    arrived = lax.all_to_all(outgoing, ("feat", "dom"), split_axis=0, concat_axis=0, tiled=True)
    return arrived.reshape(parts_total * slot_count, width)


def boundary_backward(outgoing):
    parts_total, slot_count, width = outgoing.shape
    arrived = lax.all_to_all(outgoing, ("feat", "dom"), split_axis=0, concat_axis=0, tiled=True)
    return arrived


def shards(
    features,
    w_self,
    w_neigh,
    gain,
    shift,
    d_hidden,
    send_rows,
    send_count,
    tile_src,
    tile_dst,
    tile_count,
    tile_vals,
):
    groups = features.shape[0]
    node_rows = features.shape[2]
    in_cols = features.shape[3]
    width = w_self.shape[1]
    tile_size = tile_vals.shape[3]
    nodes_total = node_rows * lax.axis_size("feat") * lax.axis_size("dom")
    local_blocks = node_rows // tile_size
    own_features = lax.all_to_all(features, "feat", split_axis=0, concat_axis=3, tiled=True)
    full_self, full_neigh = (
        lax.all_gather(w_self, "feat", axis=0, tiled=True),
        lax.all_gather(w_neigh, "feat", axis=0, tiled=True),
    )
    own_features = own_features.reshape(node_rows, in_cols * groups)
    own = jnp.dot(own_features, full_self, preferred_element_type=jnp.float32)
    far = jnp.dot(own_features, full_neigh, preferred_element_type=jnp.float32)
    neigh = far.astype(jnp.bfloat16)
    targets = send_rows[0, 0]
    parts_total, slot_count = targets.shape
    live_slot = jnp.arange(slot_count)[None, :] < send_count[0, 0][:, None]
    outgoing = jnp.where(live_slot[:, :, None], neigh[targets], jnp.zeros((), jnp.bfloat16))
    halo = boundary_forward(outgoing)
    source = jnp.concatenate([neigh, halo], axis=0).reshape(-1, tile_size, width)
    source_blocks = source.shape[0]
    values = tile_vals[0, 0]
    tile_from = tile_src[0, 0]
    tile_into = tile_dst[0, 0]
    live_tiles = tile_count[0, 0]
    turn_total = (live_tiles + per_turn - 1) // per_turn

    def turn_slices(which_turn):
        first_tile = which_turn * per_turn
        block_values = lax.dynamic_slice_in_dim(values, first_tile, per_turn, 0)
        block_from = lax.dynamic_slice_in_dim(tile_from, first_tile, per_turn, 0)
        block_into = lax.dynamic_slice_in_dim(tile_into, first_tile, per_turn, 0)
        active = (first_tile + jnp.arange(per_turn) < live_tiles).astype(jnp.float32)
        return (block_values, block_from, block_into, active)

    def forward_turn(which_turn, running):
        summed, weight_sum = running
        block_values, block_from, block_into, active = turn_slices(which_turn)
        products = jnp.einsum(
            "tij,tjh->tih", block_values, source[block_from], preferred_element_type=jnp.float32
        )
        summed = summed.at[block_into].add(products * active[:, None, None])
        row_sums = jnp.sum(block_values, axis=2, dtype=jnp.float32)
        weight_sum = weight_sum.at[block_into].add(row_sums * active[:, None])
        return (summed, weight_sum)

    start_state = (
        jnp.zeros((local_blocks, tile_size, width), jnp.float32),
        jnp.zeros((local_blocks, tile_size), jnp.float32),
    )
    summed, weight_sum = lax.fori_loop(0, turn_total, forward_turn, start_state)
    degree = 1.0 + weight_sum.reshape(node_rows)
    pre = own + summed.reshape(node_rows, width) / degree[:, None]
    column_sum, squares = lax.psum(
        (jnp.sum(pre, axis=0), jnp.sum(pre * pre, axis=0)), ("feat", "dom")
    )
    mean_pre = column_sum / nodes_total
    variance = squares / nodes_total - mean_pre * mean_pre
    inverse = 1.0 / jnp.sqrt(variance + epsilon)
    normed = (pre - mean_pre) * inverse
    act = gain * normed + shift
    logistic = jax.nn.sigmoid(act)
    hidden = (act * logistic).astype(jnp.bfloat16)
    slope = d_hidden[0, 0].astype(jnp.float32) * logistic * (1.0 + act * (1.0 - logistic))
    slope_sum, product_sum = lax.psum(
        (jnp.sum(slope, axis=0), jnp.sum(slope * normed, axis=0)), ("feat", "dom")
    )
    shift_grad = slope_sum / nodes_total
    gain_grad = product_sum / nodes_total
    dpre = gain * inverse * (slope - shift_grad - normed * gain_grad)
    message_grad = (
        (dpre / degree[:, None]).astype(jnp.bfloat16).reshape(local_blocks, tile_size, width)
    )

    def backward_turn(which_turn, running):
        block_values, block_from, block_into, active = turn_slices(which_turn)
        products = jnp.einsum(
            "tij,tih->tjh",
            block_values,
            message_grad[block_into],
            preferred_element_type=jnp.float32,
        )
        return running.at[block_from].add(products * active[:, None, None])

    source_grad = lax.fori_loop(
        0, turn_total, backward_turn, jnp.zeros((source_blocks, tile_size, width), jnp.float32)
    )
    source_grad = source_grad.reshape(-1, width)
    local_grad = source_grad[:node_rows]
    halo_grad = source_grad[node_rows:].astype(jnp.bfloat16).reshape(parts_total, slot_count, width)
    returned = boundary_backward(halo_grad)
    returned = jnp.where(
        live_slot[:, :, None], returned.astype(jnp.float32), jnp.zeros((), jnp.float32)
    )
    neigh_grad = local_grad.at[targets.reshape(-1)].add(returned.reshape(-1, width))
    out_shape = (1, 1, node_rows, width)
    return (
        hidden.reshape(out_shape),
        dpre.astype(jnp.bfloat16).reshape(out_shape),
        neigh_grad.astype(jnp.bfloat16).reshape(out_shape),
        gain_grad,
        shift_grad,
    )


def solution(mesh):
    in_specs = (
        P(None, "dom", None, "feat"),
        P("feat", None),
        P("feat", None),
        P(),
        P(),
        P("feat", "dom", None, None),
        P("feat", "dom", None, None),
        P("feat", "dom", None),
        P("feat", "dom", None),
        P("feat", "dom", None),
        P("feat", "dom"),
        P("feat", "dom", None, None, None),
    )
    out_specs = (
        P("feat", "dom", None, None),
        P("feat", "dom", None, None),
        P("feat", "dom", None, None),
        P(),
        P(),
    )
    return jax.shard_map(shards, mesh=mesh, in_specs=in_specs, out_specs=out_specs, check_vma=False)
```

profile of v0, /device:TPU:0, one launch (start us, length us, event | category | flops | bytes accessed | tf_op | source)
XLA Modules:
  0.0 451.1 jit_solution(3260794556745349745)
XLA Ops:
  0.6 2.3 copy.22
  2.9 5.3 %all-to-all-start = ((bf16[4,1,512,256]{2,3,1,0:T(8,128)(2,1)}), bf16[4,1,512,256]{2,3,1,0:T(8,128)(2,1)S(1)}, u32[]{:S(2)}, u32[]{:S(2)}) async-start(bf16[4,1,512,256]{2,3,1,0:T(8,128)(2,1)} %copy.22), calls=%async_computation | async-start | bytes 2097152 | tf_op jit(solution)/shard_map/all_to_all | solution.py:43
  8.3 19.4 %all_gather.7 = bf16[1024,256]{1,0:T(8,128)(2,1)S(1)} all-gather(bf16[256,256]{1,0:T(8,128)(2,1)S(1)} %copy-done.1), channel_id=1, replica_groups=mesh['feat'=4,'dom'=8] {'feat'}, dimensions={0}, use_global_device_ids=true | all-gather | bytes 655360 | tf_op jit(solution)/shard_map/all_gather | solution.py:46
  28.3 3.9 gather_fusion.2
  33.2 4.9 %all-to-all-start.1 = ((bf16[32,32,256]{2,1,0:T(8,128)(2,1)}), bf16[32,32,256]{2,1,0:T(8,128)(2,1)S(1)}, u32[]{:S(2)}, u32[]{:S(2)}) async-start(bf16[32,32,256]{2,1,0:T(8,128)(2,1)} %broadcast_select_fusion), calls=%async_computation.1 | async-start | bytes 1048576 | tf_op jit(solution)/shard_map/all_to_all | solution.py:12
  38.8 6.5 %copy.23 = bf16[1,1,136,128,128]{3,4,2,1,0:T(8,128)(2,1)} copy(bf16[1,1,136,128,128]{4,3,2,1,0:T(8,128)(2,1)} %param.27) | data formatting | bytes 8912896 | tf_op args[11]
  45.4 12.0 %all_gather.6 = bf16[1024,256]{1,0:T(8,128)(2,1)} all-gather(bf16[256,256]{1,0:T(8,128)(2,1)S(1)} %copy-done.2), channel_id=1, replica_groups=mesh['feat'=4,'dom'=8] {'feat'}, dimensions={0}, use_global_device_ids=true | all-gather | bytes 655360 | tf_op jit(solution)/shard_map/all_gather | solution.py:45
  57.6 100.2 %while.22 = (s32[]{:T(128)}, f32[4,128,256]{2,1,0:T(8,128)S(1)}, f32[4,128]{1,0:T(4,128)S(1)}, s32[]{:T(128)}, s32[136]{0:T(256)S(1)}, /*index=5*/bf16[136,128,1...) while((s32[]{:T(128)}, f32[4,128,256]{2,1,0:T(8,128)S(1)}, ...), condition=%wide.region_4.5_spmd, body=%wide.region_0.4_spmd.sunk | while | flops 33949224 | bytes 3156823 | solution.py:88
  58.9 1.1 convolution_multiply_fusion.4
  60.9 1.0 convert_reduce_fusion.2
  63.9 1.1 convolution_multiply_fusion.4
  65.9 1.0 convert_reduce_fusion.2
  68.9 1.1 convolution_multiply_fusion.4
  70.9 1.0 convert_reduce_fusion.2
  73.9 1.1 convolution_multiply_fusion.4
  75.9 1.0 convert_reduce_fusion.2
  78.9 1.1 convolution_multiply_fusion.4
  80.9 1.0 convert_reduce_fusion.2
  83.9 1.1 convolution_multiply_fusion.4
  89.0 1.1 convolution_multiply_fusion.4
  94.0 1.1 convolution_multiply_fusion.4
  99.0 1.1 convolution_multiply_fusion.4
  101.0 1.0 convert_reduce_fusion.2
  104.0 1.1 convolution_multiply_fusion.4
  109.0 1.1 convolution_multiply_fusion.4
  111.0 1.0 convert_reduce_fusion.2
  114.0 1.1 convolution_multiply_fusion.4
  119.0 1.1 convolution_multiply_fusion.4
  121.0 1.0 convert_reduce_fusion.2
  124.0 1.1 convolution_multiply_fusion.4
  129.0 1.1 convolution_multiply_fusion.4
  134.0 1.1 convolution_multiply_fusion.4
  139.1 1.1 convolution_multiply_fusion.4
  144.1 1.1 convolution_multiply_fusion.4
  149.1 1.1 convolution_multiply_fusion.4
  154.1 1.1 convolution_multiply_fusion.4
  158.0 1.6 fusion.11
  159.5 107.0 %all-reduce.1 = (f32[256]{0:T(256)S(1)}, f32[256]{0:T(256)S(1)}) all-reduce(f32[256]{0:T(256)S(1)} %get-tuple-element.130, f32[256]{0:T(256)S(1)} %get-tuple-element.129), channel_id=1, replica_groups=mesh['feat'=4,'dom'=8] {'feat','dom'}, use_global_device_ids=true, to_apply=%region_8.9 | all-reduce | flops 512 | bytes 4096 | tf_op jit(solution)/shard_map/psum | solution.py:91
  266.9 41.7 %all-reduce = (f32[256]{0:T(256)S(1)}, f32[256]{0:T(256)S(1)}) all-reduce(f32[256]{0:T(256)S(1)} %get-tuple-element.128, f32[256]{0:T(256)S(1)} %get-tuple-element.127), channel_id=1, replica_groups=mesh['feat'=4,'dom'=8] {'feat','dom'}, use_global_device_ids=true, to_apply=%region_12.13 | all-reduce | flops 512 | bytes 4096 | tf_op jit(solution)/shard_map/psum | solution.py:102
  308.6 1.2 divide_convert_fusion
  309.9 67.2 %while.23 = (s32[]{:T(128)}, f32[12,128,256]{2,1,0:T(8,128)S(1)}, s32[]{:T(128)}, s32[136]{0:T(256)S(1)}, bf16[136,128,128]{1,2,0:T(8,128)(2,1)}, /*index=5*/s32...) while((s32[]{:T(128)}, f32[12,128,256]{2,1,0:T(8,128)S(1)}, ...), condition=%wide.region_15.16_spmd, body=%wide.region_13.15_spmd.sunk | while | flops 33817640 | bytes 3019083 | solution.py:122
  311.3 1.1 convolution_multiply_fusion.5
  314.6 1.1 convolution_multiply_fusion.5
  318.0 1.1 convolution_multiply_fusion.5
  321.3 1.1 convolution_multiply_fusion.5
  324.7 1.1 convolution_multiply_fusion.5
  328.1 1.1 convolution_multiply_fusion.5
  331.4 1.1 convolution_multiply_fusion.5
  334.8 1.1 convolution_multiply_fusion.5
  338.2 1.1 convolution_multiply_fusion.5
  341.5 1.1 convolution_multiply_fusion.5
  344.9 1.1 convolution_multiply_fusion.5
  348.2 1.1 convolution_multiply_fusion.5
  351.6 1.1 convolution_multiply_fusion.5
  354.9 1.1 convolution_multiply_fusion.5
  358.3 1.1 convolution_multiply_fusion.5
  361.7 1.1 convolution_multiply_fusion.5
  365.0 1.1 convolution_multiply_fusion.5
  368.4 1.1 convolution_multiply_fusion.5
  371.7 1.1 convolution_multiply_fusion.5
  375.1 1.1 convolution_multiply_fusion.5
  378.0 49.7 %all-to-all-start.2 = ((bf16[32,32,256]{2,1,0:T(8,128)(2,1)}), bf16[32,32,256]{2,1,0:T(8,128)(2,1)S(1)}, u32[]{:S(2)}, u32[]{:S(2)}) async-start(bf16[32,32,256]{2,1,0:T(8,128)(2,1)} %bitcast.23), calls=%async_computation.2 | async-start | bytes 1048576 | tf_op jit(solution)/shard_map/all_to_all | solution.py:18
  427.8 16.1 %all-to-all-done.2 = bf16[32,32,256]{2,1,0:T(8,128)(2,1)S(1)} async-done(((bf16[32,32,256]{2,1,0:T(8,128)(2,1)}), bf16[32,32,256]{2,1,0:T(8,128)(2,1)S(1)}, u32[]{:S(2)}, u32[]{:S(2)}) %all-to-all-start.2) | async-done | bytes 524320 | tf_op jit(solution)/shard_map/all_to_all | solution.py:18
  444.1 6.3 %scatter_fusion.2 = f32[512,256]{1,0:T(8,128)S(1)} fusion(f32[512,256]{1,0:T(8,128)S(1)} %bitcast.57, s32[1024]{0:T(1024)S(1)} %bitcast.69, f32[1024,256]{1,0:T(8,128)S(1)} %bitcast.62), kind=kCustom, calls=%fused_computation.6 | custom fusion | flops 262144 | bytes 3149824 | tf_op jit(solution)/shard_map/scatter-add | solution.py:132
  (277 shorter events, 116.7 us)
Async XLA Ops:
  0.6 7.6 %copy-start.3 = (s32[1,1,32,32]{3,2,1,0:T(8,128)S(1)}, s32[1,1,32,32]{3,2,1,0:T(8,128)}, u32[]{:S(2)}) copy-start(s32[1,1,32,32]{3,2,1,0:T(8,128)} %param.22) | copy-start | bytes 12292
  2.9 5.4 %copy-start.1 = (bf16[256,256]{1,0:T(8,128)(2,1)S(1)}, bf16[256,256]{1,0:T(8,128)(2,1)}, u32[]{:S(2)}) copy-start(bf16[256,256]{1,0:T(8,128)(2,1)} %param.18) | copy-start | bytes 393220
  2.9 24.8 %copy-start.10 = (s32[1,1,32]{2,1,0:T(1,128)S(1)}, s32[1,1,32]{2,1,0:T(1,128)}, u32[]{:S(2)}) copy-start(s32[1,1,32]{2,1,0:T(1,128)} %param.23) | copy-start | bytes 388
  2.9 24.9 %all-to-all-start = ((bf16[4,1,512,256]{2,3,1,0:T(8,128)(2,1)}), bf16[4,1,512,256]{2,3,1,0:T(8,128)(2,1)S(1)}, u32[]{:S(2)}, u32[]{:S(2)}) async-start(bf16[4,1,512,256]{2,3,1,0:T(8,128)(2,1)} %copy.22), calls=%async_computation | async-start | bytes 2097152 | tf_op jit(solution)/shard_map/all_to_all | solution.py:43
  33.2 24.2 %all-to-all-start.1 = ((bf16[32,32,256]{2,1,0:T(8,128)(2,1)}), bf16[32,32,256]{2,1,0:T(8,128)(2,1)S(1)}, u32[]{:S(2)}, u32[]{:S(2)}) async-start(bf16[32,32,256]{2,1,0:T(8,128)(2,1)} %broadcast_select_fusion), calls=%async_computation.1 | async-start | bytes 1048576 | tf_op jit(solution)/shard_map/all_to_all | solution.py:12
  38.8 6.6 %copy-start.2 = (bf16[256,256]{1,0:T(8,128)(2,1)S(1)}, bf16[256,256]{1,0:T(8,128)(2,1)}, u32[]{:S(2)}) copy-start(bf16[256,256]{1,0:T(8,128)(2,1)} %param.17) | copy-start | bytes 393220
  45.4 12.2 %copy-start.4 = (s32[1,1,136]{2,1,0:T(1,128)S(1)}, s32[1,1,136]{2,1,0:T(1,128)}, u32[]{:S(2)}) copy-start(s32[1,1,136]{2,1,0:T(1,128)} %param.25) | copy-start | bytes 1636
  45.4 12.2 %copy-start.5 = (s32[1,1,136]{2,1,0:T(1,128)S(1)}, s32[1,1,136]{2,1,0:T(1,128)}, u32[]{:S(2)}) copy-start(s32[1,1,136]{2,1,0:T(1,128)} %param.24) | copy-start | bytes 1636
  157.9 108.6 %copy-start.6 = (f32[256]{0:T(256)S(1)}, f32[256]{0:T(256)}, u32[]{:S(2)}) copy-start(f32[256]{0:T(256)} %param.19) | copy-start | bytes 3076
  157.9 108.6 %copy-start = (bf16[1,1,512,256]{3,2,1,0:T(8,128)(2,1)S(1)}, bf16[1,1,512,256]{3,2,1,0:T(8,128)(2,1)}, u32[]{:S(2)}) copy-start(bf16[1,1,512,256]{3,2,1,0:T(8,128)(2,1)} %param.21) | copy-start | bytes 786436
  157.9 108.6 %copy-start.7 = (f32[256]{0:T(256)S(1)}, f32[256]{0:T(256)}, u32[]{:S(2)}) copy-start(f32[256]{0:T(256)} %param.20) | copy-start | bytes 3076
  308.5 1.3 copy-start.8
  308.6 1.4 copy-start.9
  378.0 65.9 %all-to-all-start.2 = ((bf16[32,32,256]{2,1,0:T(8,128)(2,1)}), bf16[32,32,256]{2,1,0:T(8,128)(2,1)S(1)}, u32[]{:S(2)}, u32[]{:S(2)}) async-start(bf16[32,32,256]{2,1,0:T(8,128)(2,1)} %bitcast.23), calls=%async_computation.2 | async-start | bytes 1048576 | tf_op jit(solution)/shard_map/all_to_all | solution.py:18
where the time goes:
time: 453 us; the launch traced here: 451 us
  blocking collectives  180 us (40%)
  other arithmetic  108 us (24%)
  starting transfers between devices  59.9 us (13%)
  matrix products  46.8 us (10%)
  local copies, waits for them, and re-layouts  36.6 us (8%)
  waiting for transfers between devices  16.1 us (4%)
    psum x1, blocking collectives, shards(): lax.psum((jnp.sum(pre, axis=0), jnp.sum(pre * pre, axis=0)), ('feat', 'do...  107 us
    all_to_all x1, starting transfers between devices, boundary_backward(): lax.all_to_all(outgoing, ('feat', 'dom'), split_axis=0, concat_axis=0, ti...  49.7 us
    psum x1, blocking collectives, shards(): lax.psum((jnp.sum(slope, axis=0), jnp.sum(slope * normed, axis=0)), ('fea...  41.7 us
    convert_element_type x40, other arithmetic, turn_slices(): (first_tile + jnp.arange(per_turn) < live_tiles).astype(jnp.float32)  26 us
    dot_general x20, matrix products, backward_turn(): jnp.einsum('tij,tih->tjh', block_values, message_grad[block_into], prefer...  22.4 us
    dot_general x20, matrix products, forward_turn(): jnp.einsum('tij,tjh->tih', block_values, source[block_from], preferred_el...  22.4 us
    reduce_sum x20, other arithmetic, forward_turn(): row_sums = jnp.sum(block_values, axis=2, dtype=jnp.float32)  20.4 us
    all_gather x1, blocking collectives, shards(): lax.all_gather(w_neigh, 'feat', axis=0, tiled=True)  19.4 us
  transfers between devices with their start and end apart: 3, of which 1 were waited for; matrix products, arithmetic and copies ran while one was open for 2% of the time, Pallas kernels for 0%

commit v1 on v0

v1 whole, which is shorter than its diff:
```python
import functools

import jax
import jax.numpy as jnp
from jax import lax
from jax.experimental import pallas as pl
from jax.experimental.pallas import tpu as pltpu
from jax.sharding import PartitionSpec as P

epsilon = 1e-05
MESH = pl.DeviceIdType.MESH
VM = pl.BlockSpec(memory_space=pltpu.VMEM)
SM = pl.BlockSpec(memory_space=pltpu.SMEM)
ANY = pl.BlockSpec(memory_space=pl.ANY)
f32 = jnp.float32
bf16 = jnp.bfloat16


def place(feat_size, dom_size):
    me_f, me_d = lax.axis_index("feat"), lax.axis_index("dom")
    me = me_f * dom_size + me_d
    total = feat_size * dom_size

    def peer_of(k):
        peer = lax.rem(me + k, total)
        return peer, (lax.div(peer, dom_size), lax.rem(peer, dom_size))

    return me_f, me_d, me, total, peer_of


def meet_all(total, peer_of):
    barrier = pltpu.get_barrier_semaphore()

    def greet(k, carry):
        _, where = peer_of(k)
        pl.semaphore_signal(barrier, inc=1, device_id=where, device_id_type=MESH)
        return carry

    lax.fori_loop(1, total, greet, 0)
    pl.semaphore_wait(barrier, total - 1)


def exchange(me, total, peer_of, source_of, target_of, send_sems, recv_sems):
    def copy_to(peer, where):
        return pltpu.make_async_remote_copy(
            src_ref=source_of(peer),
            dst_ref=target_of(me),
            send_sem=send_sems.at[peer],
            recv_sem=recv_sems.at[me],
            device_id=where,
            device_id_type=MESH,
        )

    def copy_from(peer, where):
        return pltpu.make_async_remote_copy(
            src_ref=source_of(peer),
            dst_ref=target_of(peer),
            send_sem=send_sems.at[peer],
            recv_sem=recv_sems.at[peer],
            device_id=where,
            device_id_type=MESH,
        )

    def begin():
        def start(k, carry):
            copy_to(*peer_of(k)).start()
            return carry

        lax.fori_loop(1, total, start, 0)

    def finish_recv():
        def wait(k, carry):
            copy_from(*peer_of(k)).wait_recv()
            return carry

        lax.fori_loop(1, total, wait, 0)

    def finish_send():
        def wait(k, carry):
            copy_to(*peer_of(k)).wait_send()
            return carry

        lax.fori_loop(1, total, wait, 0)

    return begin, finish_recv, finish_send


def selection(rows_ref, count_ref, node_rows):
    rows = rows_ref[0, 0]
    parts, slots = rows.shape
    counts = jnp.broadcast_to(count_ref[0], (slots, parts)).T
    live = lax.broadcasted_iota(jnp.int32, (parts, slots), 1) < counts
    wanted = jnp.where(live, rows, -1)
    nodes = lax.broadcasted_iota(jnp.int32, (parts, slots, node_rows), 2)
    picked = wanted[:, :, None] == nodes
    return jnp.where(picked, 1.0, 0.0).astype(bf16).reshape(parts * slots, node_rows)


def project_kernel(feat_size, dom_size, x_ref, ws_ref, wn_ref, rows_ref, count_ref,
                   own_ref, source_ref, xbuf, wnbuf, wsbuf, acc, pick, outgoing,
                   local_sems, near_send, near_recv, far_send, far_recv):
    me_f, me_d, me, total, peer_of = place(feat_size, dom_size)
    node_rows = x_ref.shape[2]
    slots = rows_ref.shape[3]
    mine = [
        pltpu.make_async_copy(wn_ref, wnbuf.at[me_f], local_sems.at[0]),
        pltpu.make_async_copy(x_ref.at[me_f, 0], xbuf.at[me_f], local_sems.at[1]),
        pltpu.make_async_copy(ws_ref, wsbuf.at[me_f], local_sems.at[2]),
    ]
    for copy in mine:
        copy.start()
    meet_all(total, peer_of)

    def near(kind, k):
        other = lax.rem(me_f + k, feat_size)
        source = (wn_ref, x_ref.at[other, 0], ws_ref)[kind]
        return pltpu.make_async_remote_copy(
            src_ref=source,
            dst_ref=(wnbuf, xbuf, wsbuf)[kind].at[me_f],
            send_sem=near_send.at[kind, other],
            recv_sem=near_recv.at[kind, me_f],
            device_id=(other, me_d),
            device_id_type=MESH,
        )

    def near_arrival(kind, k):
        other = lax.rem(me_f + k, feat_size)
        source = (wn_ref, x_ref.at[other, 0], ws_ref)[kind]
        return pltpu.make_async_remote_copy(
            src_ref=source,
            dst_ref=(wnbuf, xbuf, wsbuf)[kind].at[other],
            send_sem=near_send.at[kind, other],
            recv_sem=near_recv.at[kind, other],
            device_id=(other, me_d),
            device_id_type=MESH,
        )

    for kind in range(3):
        for k in range(1, feat_size):
            near(kind, k).start()
    pick[...] = selection(rows_ref, count_ref, node_rows)
    mine[0].wait()
    mine[1].wait()
    acc[...] = jnp.dot(xbuf[me_f], wnbuf[me_f], preferred_element_type=f32)
    for k in range(1, feat_size):
        near_arrival(0, k).wait_recv()
        near_arrival(1, k).wait_recv()
        other = lax.rem(me_f + k, feat_size)
        acc[...] += jnp.dot(xbuf[other], wnbuf[other], preferred_element_type=f32)
    neigh = acc[...].astype(bf16)
    source_ref[0:node_rows] = neigh
    outgoing[...] = jnp.dot(pick[...], neigh, preferred_element_type=f32).astype(bf16)

    def out_rows(peer):
        return outgoing.at[pl.ds(pl.multiple_of(peer * slots, slots), slots)]

    def in_rows(peer):
        return source_ref.at[pl.ds(pl.multiple_of(node_rows + peer * slots, slots), slots)]

    begin, finish_recv, finish_send = exchange(me, total, peer_of, out_rows, in_rows, far_send, far_recv)
    begin()
    source_ref[pl.ds(pl.multiple_of(node_rows + me * slots, slots), slots)] = outgoing[
        pl.ds(pl.multiple_of(me * slots, slots), slots)
    ]
    mine[2].wait()
    own_ref[...] = jnp.dot(xbuf[me_f], wsbuf[me_f], preferred_element_type=f32)
    for k in range(1, feat_size):
        near_arrival(2, k).wait_recv()
        other = lax.rem(me_f + k, feat_size)
        own_ref[...] += jnp.dot(xbuf[other], wsbuf[other], preferred_element_type=f32)
    for kind in range(3):
        for k in range(1, feat_size):
            near(kind, k).wait_send()
    finish_recv()
    finish_send()


def load_turns(vals_ref, vbuf, sems, turns, per_turn):
    def chunk(i):
        span = pl.ds(i * per_turn, per_turn)
        return pltpu.make_async_copy(vals_ref.at[0, 0, span], vbuf.at[span], sems.at[i])

    def start(i, carry):
        chunk(i).start()
        return carry

    lax.fori_loop(0, turns, start, 0)
    return chunk


def gather_kernel(per_turn, own_ref, source_ref, from_ref, into_ref, count_ref, vals_ref,
                  pre_ref, scale_ref, stats_ref, acc, weight, vbuf, sems):
    blocks = acc.shape[0] - 1
    tile = acc.shape[1]
    live = count_ref[0, 0]
    turns = lax.div(live + per_turn - 1, per_turn)
    chunk = load_turns(vals_ref, vbuf, sems, turns, per_turn)
    acc[...] = jnp.zeros_like(acc)
    weight[...] = jnp.zeros_like(weight)

    def turn(i, carry):
        chunk(i).wait()
        products = []
        for j in range(per_turn):
            t = i * per_turn + j
            products.append(jnp.dot(vbuf[t], source_ref[from_ref[0, 0, t]], preferred_element_type=f32))
        for j in range(per_turn):
            t = i * per_turn + j
            into = jnp.where(t < live, into_ref[0, 0, t], blocks)
            acc[into] += products[j]
            weight[into] += vbuf[t].astype(f32)
        return carry

    lax.fori_loop(0, turns, turn, 0)
    total = jnp.zeros((1, acc.shape[2]), f32)
    squares = jnp.zeros((1, acc.shape[2]), f32)
    for b in range(blocks):
        degree = 1.0 + jnp.sum(weight[b], axis=1, keepdims=True)
        inverse = 1.0 / degree
        span = slice(b * tile, (b + 1) * tile)
        pre = own_ref[span] + acc[b] * inverse
        pre_ref[span] = pre
        scale_ref[span] = jnp.broadcast_to(inverse, (tile, 128))
        total += jnp.sum(pre, axis=0, keepdims=True)
        squares += jnp.sum(pre * pre, axis=0, keepdims=True)
    stats_ref[0:1] = total
    stats_ref[1:2] = squares


def norm_kernel(feat_size, dom_size, tile, pre_ref, scale_ref, stats_ref, gain_ref, shift_ref, dh_ref,
                hidden_ref, dself_ref, mg_ref, ggrad_ref, sgrad_ref,
                normed_buf, slope_buf, first, second, local, send1, recv1, send2, recv2):
    me_f, me_d, me, total, peer_of = place(feat_size, dom_size)
    node_rows, width = pre_ref.shape
    nodes = node_rows * total
    blocks = node_rows // tile
    first[me] = stats_ref[...]
    meet_all(total, peer_of)
    begin, finish_recv, finish_send1 = exchange(
        me, total, peer_of, lambda peer: stats_ref, lambda peer: first.at[peer], send1, recv1)
    begin()
    finish_recv()
    sums = jnp.sum(first[...], axis=0)
    mean = sums[0:1] / nodes
    variance = sums[1:2] / nodes - mean * mean
    inverse = 1.0 / jnp.sqrt(variance + epsilon)
    gain = gain_ref[...].reshape(1, width)
    shift = shift_ref[...].reshape(1, width)
    slope_sum = jnp.zeros((1, width), f32)
    product_sum = jnp.zeros((1, width), f32)
    for b in range(blocks):
        span = slice(b * tile, (b + 1) * tile)
        normed = (pre_ref[span] - mean) * inverse
        act = gain * normed + shift
        logistic = jax.nn.sigmoid(act)
        hidden_ref[span] = (act * logistic).astype(bf16)
        slope = dh_ref[0, 0, span].astype(f32) * logistic * (1.0 + act * (1.0 - logistic))
        normed_buf[span] = normed
        slope_buf[span] = slope
        slope_sum += jnp.sum(slope, axis=0, keepdims=True)
        product_sum += jnp.sum(slope * normed, axis=0, keepdims=True)
    local[0:1] = slope_sum
    local[1:2] = product_sum
    second[me] = local[...]
    begin, finish_recv, finish_send2 = exchange(
        me, total, peer_of, lambda peer: local, lambda peer: second.at[peer], send2, recv2)
    begin()
    finish_recv()
    sums = jnp.sum(second[...], axis=0)
    shift_grad = sums[0:1] / nodes
    gain_grad = sums[1:2] / nodes
    sgrad_ref[...] = shift_grad
    ggrad_ref[...] = gain_grad
    factor = gain * inverse
    for b in range(blocks):
        span = slice(b * tile, (b + 1) * tile)
        dpre = factor * (slope_buf[span] - shift_grad - normed_buf[span] * gain_grad)
        dself_ref[span] = dpre.astype(bf16)
        mg_ref[b] = (dpre * scale_ref[span, 0:1]).astype(bf16)
    finish_send1()
    finish_send2()


def spread_kernel(per_turn, own_blocks, mg_ref, from_ref, into_ref, count_ref, vals_ref,
                  near_ref, halo_ref, acc, vbuf, sems):
    blocks = acc.shape[0] - 1
    live = count_ref[0, 0]
    turns = lax.div(live + per_turn - 1, per_turn)
    chunk = load_turns(vals_ref, vbuf, sems, turns, per_turn)
    acc[...] = jnp.zeros_like(acc)

    def turn(i, carry):
        chunk(i).wait()
        products = []
        for j in range(per_turn):
            t = i * per_turn + j
            products.append(lax.dot_general(
                vbuf[t], mg_ref[into_ref[0, 0, t]], (((0,), (0,)), ((), ())), preferred_element_type=f32))
        for j in range(per_turn):
            t = i * per_turn + j
            origin = jnp.where(t < live, from_ref[0, 0, t], blocks)
            acc[origin] += products[j]
        return carry

    lax.fori_loop(0, turns, turn, 0)
    near_ref[...] = acc[0:own_blocks]
    halo_ref[...] = acc[own_blocks:blocks].astype(bf16)


def return_kernel(feat_size, dom_size, near_ref, halo_ref, rows_ref, count_ref,
                  out_ref, returned, pick, send, recv):
    me_f, me_d, me, total, peer_of = place(feat_size, dom_size)
    slots = rows_ref.shape[3]
    node_rows = near_ref.shape[0]

    def rows_of(ref):
        return lambda peer: ref.at[pl.ds(pl.multiple_of(peer * slots, slots), slots)]

    returned[pl.ds(pl.multiple_of(me * slots, slots), slots)] = halo_ref[
        pl.ds(pl.multiple_of(me * slots, slots), slots)
    ]
    meet_all(total, peer_of)
    begin, finish_recv, finish_send = exchange(
        me, total, peer_of, rows_of(halo_ref), rows_of(returned), send, recv)
    begin()
    pick[...] = selection(rows_ref, count_ref, node_rows)
    finish_recv()
    added = lax.dot_general(pick[...], returned[...], (((0,), (0,)), ((), ())), preferred_element_type=f32)
    out_ref[...] = (near_ref[...] + added).astype(bf16)
    finish_send()


def shards(feat_size, dom_size, features, w_self, w_neigh, gain, shift, d_hidden, send_rows, send_count,
           tile_src, tile_dst, tile_count, tile_vals):
    node_rows, columns = features.shape[2], features.shape[3]
    width = w_self.shape[1]
    tiles, tile = tile_vals.shape[2], tile_vals.shape[3]
    parts, slots = send_rows.shape[2], send_rows.shape[3]
    own_blocks = node_rows // tile
    halo_rows = parts * slots
    blocks = (node_rows + halo_rows) // tile
    per_turn = next(n for n in (8, 4, 2, 1) if tiles % n == 0)
    turns = tiles // per_turn
    dma = pltpu.SemaphoreType.DMA
    shape = jax.ShapeDtypeStruct
    big = 60 * 1024 * 1024

    def remote(number):
        return pltpu.CompilerParams(collective_id=number, has_side_effects=True, vmem_limit_bytes=big)

    own, source = pl.pallas_call(
        functools.partial(project_kernel, feat_size, dom_size),
        out_shape=(shape((node_rows, width), f32), shape((node_rows + halo_rows, width), bf16)),
        in_specs=[ANY, ANY, ANY, VM, VM],
        out_specs=(VM, VM),
        scratch_shapes=[
            pltpu.VMEM((feat_size, node_rows, columns), bf16),
            pltpu.VMEM((feat_size, columns, width), bf16),
            pltpu.VMEM((feat_size, columns, width), bf16),
            pltpu.VMEM((node_rows, width), f32),
            pltpu.VMEM((halo_rows, node_rows), bf16),
            pltpu.VMEM((halo_rows, width), bf16),
            dma((3,)), dma((3, feat_size)), dma((3, feat_size)), dma((parts,)), dma((parts,)),
        ],
        compiler_params=remote(0),
        name="project",
    )(features, w_self, w_neigh, send_rows, send_count)
    pre, scale, stats = pl.pallas_call(
        functools.partial(gather_kernel, per_turn),
        out_shape=(shape((node_rows, width), f32), shape((node_rows, 128), f32), shape((2, width), f32)),
        in_specs=[VM, VM, SM, SM, SM, ANY],
        out_specs=(VM, VM, VM),
        scratch_shapes=[
            pltpu.VMEM((own_blocks + 1, tile, width), f32),
            pltpu.VMEM((own_blocks + 1, tile, tile), f32),
            pltpu.VMEM((tiles, tile, tile), bf16),
            dma((turns,)),
        ],
        compiler_params=pltpu.CompilerParams(vmem_limit_bytes=big),
        name="gather",
    )(own, source.reshape(blocks, tile, width), tile_src, tile_dst, tile_count, tile_vals)
    hidden, d_self, message_grad, gain_grad, shift_grad = pl.pallas_call(
        functools.partial(norm_kernel, feat_size, dom_size, tile),
        out_shape=(
            shape((node_rows, width), bf16),
            shape((node_rows, width), bf16),
            shape((own_blocks, tile, width), bf16),
            shape((1, width), f32),
            shape((1, width), f32),
        ),
        in_specs=[VM] * 6,
        out_specs=(VM,) * 5,
        scratch_shapes=[
            pltpu.VMEM((node_rows, width), f32),
            pltpu.VMEM((node_rows, width), f32),
            pltpu.VMEM((parts, 2, width), f32),
            pltpu.VMEM((parts, 2, width), f32),
            pltpu.VMEM((2, width), f32),
            dma((parts,)), dma((parts,)), dma((parts,)), dma((parts,)),
        ],
        compiler_params=remote(1),
        name="norm",
    )(pre, scale, stats, gain, shift, d_hidden)
    near, halo = pl.pallas_call(
        functools.partial(spread_kernel, per_turn, own_blocks),
        out_shape=(
            shape((own_blocks, tile, width), f32),
            shape((blocks - own_blocks, tile, width), bf16),
        ),
        in_specs=[VM, SM, SM, SM, ANY],
        out_specs=(VM, VM),
        scratch_shapes=[
            pltpu.VMEM((blocks + 1, tile, width), f32),
            pltpu.VMEM((tiles, tile, tile), bf16),
            dma((turns,)),
        ],
        compiler_params=pltpu.CompilerParams(vmem_limit_bytes=big),
        name="spread",
    )(message_grad, tile_src, tile_dst, tile_count, tile_vals)
    d_neigh = pl.pallas_call(
        functools.partial(return_kernel, feat_size, dom_size),
        out_shape=shape((node_rows, width), bf16),
        in_specs=[VM] * 4,
        out_specs=VM,
        scratch_shapes=[
            pltpu.VMEM((halo_rows, width), bf16),
            pltpu.VMEM((halo_rows, node_rows), bf16),
            dma((parts,)), dma((parts,)),
        ],
        compiler_params=remote(2),
        name="giveback",
    )(near.reshape(node_rows, width), halo.reshape(halo_rows, width), send_rows, send_count)
    out_shape = (1, 1, node_rows, width)
    return (
        hidden.reshape(out_shape),
        d_self.reshape(out_shape),
        d_neigh.reshape(out_shape),
        gain_grad.reshape(width),
        shift_grad.reshape(width),
    )


def solution(mesh):
    in_specs = (
        P(None, "dom", None, "feat"),
        P("feat", None),
        P("feat", None),
        P(),
        P(),
        P("feat", "dom", None, None),
        P("feat", "dom", None, None),
        P("feat", "dom", None),
        P("feat", "dom", None),
        P("feat", "dom", None),
        P("feat", "dom"),
        P("feat", "dom", None, None, None),
    )
    out_specs = (
        P("feat", "dom", None, None),
        P("feat", "dom", None, None),
        P("feat", "dom", None, None),
        P(),
        P(),
    )
    body = functools.partial(shards, mesh.shape["feat"], mesh.shape["dom"])
    return jax.shard_map(body, mesh=mesh, in_specs=in_specs, out_specs=out_specs, check_vma=False)
```

time: 453 us -> 102 us (0.23)
  blocking collectives: 180 us -> 0 us
  other arithmetic: 108 us -> 0 us
  Pallas kernels: 0 us -> 95.1 us
  starting transfers between devices: 59.9 us -> 0 us
  matrix products: 46.8 us -> 0 us
  local copies, waits for them, and re-layouts: 36.6 us -> 4.22 us
  waiting for transfers between devices: 16.1 us -> 0 us
    psum x2 -> x0, blocking collectives: 149 us -> none  [the longest x1 107 us: shards(): lax.psum((jnp.sum(pre, axis=0), jnp.sum(pre * pre, axis=0)), ('feat', 'do...]
    pallas_call x0 -> x5, Pallas kernels: none -> 95.1 us  [the longest x1 42.4 us: shards(): pl.pallas_call(functools.partial(project_kernel, feat_size, dom_size), ou...]
    all_to_all x3 -> x0, starting transfers between devices: 59.9 us -> none  [the longest x1 49.7 us: boundary_backward(): lax.all_to_all(outgoing, ('feat', 'dom'), split_axis=0, concat_axis=0, ti...]
    scatter-add x61 -> x0, other arithmetic: 54.3 us -> none  [the longest x20 17.7 us: backward_turn(): return running.at[block_from].add(products * active[:, None, None])]
    dot_general x42 -> x0, matrix products: 46.8 us -> none  [the longest x20 22.4 us: backward_turn(): jnp.einsum('tij,tih->tjh', block_values, message_grad[block_into], prefer...]
    all_gather x2 -> x0, blocking collectives: 31.4 us -> none  [the longest x1 19.4 us: shards(): lax.all_gather(w_neigh, 'feat', axis=0, tiled=True)]
    convert_element_type x41 -> x0, other arithmetic: 27.2 us -> none  [the longest x40 26 us: turn_slices(): (first_tile + jnp.arange(per_turn) < live_tiles).astype(jnp.float32)]
    gather x41 -> x0, local copies, waits for them, and re-layouts: 26.5 us -> none  [the longest x20 11.3 us: forward_turn(): source[block_from]]
  transfers between devices with their start and end apart: 3 -> 0, of which waited for: 1 -> 0; matrix products, arithmetic and copies ran while one was open for 2% -> 0% of each run, Pallas kernels for 0% -> 0%
where the time goes in v1:
time: 102 us; the launch traced here: 101 us
  Pallas kernels  95.1 us (93%)
  local copies, waits for them, and re-layouts  4.22 us (4%)
  between operations  1.36 us (1%)
    pallas_call x1, Pallas kernels, shards(): pl.pallas_call(functools.partial(project_kernel, feat_size, dom_size), ou...  42.4 us
    pallas_call x1, Pallas kernels, shards(): pl.pallas_call(functools.partial(return_kernel, feat_size, dom_size), out...  20.4 us
    pallas_call x1, Pallas kernels, shards(): pl.pallas_call(functools.partial(norm_kernel, feat_size, dom_size, tile),...  19.8 us
    pallas_call x1, Pallas kernels, shards(): pl.pallas_call(functools.partial(gather_kernel, per_turn), out_shape=(sha...  6.42 us
    pallas_call x1, Pallas kernels, shards(): pl.pallas_call(functools.partial(spread_kernel, per_turn, own_blocks), ou...  6.17 us
    unnamed x13, local copies, waits for them, and re-layouts  4.22 us

profile of v1, /device:TPU:0, one launch (start us, length us, event | category | flops | bytes accessed | tf_op | source)
XLA Modules:
  0.0 100.7 jit_solution(18024163061544964920)
XLA Ops:
  1.3 42.4 %project.1 = (f32[512,256]{1,0:T(8,128)}, bf16[1536,256]{1,0:T(8,128)(2,1)}) custom-call(bf16[4,1,512,256]{3,2,1,0:T(8,128)(2,1)} %x_ref.1, bf16[256,256]{1,0:T(8,128)(2,1)} %ws_ref.1, bf16[256,256]{1,0:T(8,128)(2,1)} %wn_ref.1, s32[1,1,32,32]{3,2,1,0:T(8,128)} %rows_ref.3, s32[1,1,32]{2,1,0:T(1,128)} %count_ref.5), custom_call_target="tpu_custom_call" | custom-call | tf_op jit(solution)/shard_map/project/pallas_call | solution.py:351
  43.6 6.4 %gather.1 = (f32[512,256]{1,0:T(8,128)}, f32[512,128]{1,0:T(8,128)}, f32[2,256]{1,0:T(2,128)}) custom-call(f32[512,256]{1,0:T(8,128)} %get-tuple-element.17.own_ref, bf16[12,128,256]{2,1,0:T(8,128)(2,1)} %bitcast.9, s32[1,1,136]{2,1,0:T(1,128)} %from_ref.3, s32[1,1,136]{2,1,0:T(1,128)} %into_ref.3, s32[1,1]{1,0:T(1,128)S(6)} %copy.22.count_ref, ...), custom_call_target="tpu_custom_call" | custom-call | tf_op jit(solution)/shard_map/gather/pallas_call | solution.py:368
  50.1 19.8 %norm.1 = (bf16[512,256]{1,0:T(8,128)(2,1)}, bf16[512,256]{1,0:T(8,128)(2,1)}, bf16[4,128,256]{2,1,0:T(8,128)(2,1)}, f32[1,256]{1,0:T(1,128)}, f32[1,256]{1,0:T(1,128)}) custom-call(f32[512,256]{1,0:T(8,128)} %get-tuple-element.19.pre_ref, f32[512,128]{1,0:T(8,128)} %get-tuple-element.20.scale_ref, f32[2,256]{1,0:T(2,128)} %get-tuple-element.21.stats_ref, ...), custom_call_target="tpu_custom_call" | custom-call | tf_op jit(solution)/shard_map/norm/pallas_call | solution.py:382
  69.9 0.0 copy-start.1
  69.9 0.0 copy-start
  69.9 0.0 copy-start.3
  69.9 0.0 copy-start.2
  69.9 6.2 %spread.1 = (f32[4,128,256]{2,1,0:T(8,128)}, bf16[8,128,256]{2,1,0:T(8,128)(2,1)}) custom-call(bf16[4,128,256]{2,1,0:T(8,128)(2,1)} %get-tuple-element.24.mg_ref, s32[1,1,136]{2,1,0:T(1,128)} %from_ref.3, s32[1,1,136]{2,1,0:T(1,128)} %into_ref.3, s32[1,1]{1,0:T(1,128)S(6)} %copy.22.count_ref, bf16[1,1,136,128,128]{4,3,2,1,0:T(8,128)(2,1)} %vals_ref.3), custom_call_target="tpu_custom_call" | custom-call | tf_op jit(solution)/shard_map/spread/pallas_call | solution.py:404
  76.1 20.4 %giveback.1 = bf16[512,256]{1,0:T(8,128)(2,1)} custom-call(f32[512,256]{1,0:T(8,128)} %bitcast.10, bf16[1024,256]{1,0:T(8,128)(2,1)} %bitcast.11, s32[1,1,32,32]{3,2,1,0:T(8,128)} %rows_ref.3, s32[1,1,32]{2,1,0:T(1,128)} %count_ref.5), custom_call_target="tpu_custom_call" | custom-call | tf_op jit(solution)/shard_map/giveback/pallas_call | solution.py:420
  96.5 0.0 copy-done.1
  96.5 0.7 copy.23
  97.2 0.0 copy-done
  97.2 0.7 copy.24
  97.9 1.7 %copy.25 = bf16[1,1,512,256]{3,2,1,0:T(8,128)(2,1)} copy(bf16[1,1,512,256]{3,2,1,0:T(8,128)(2,1)} %bitcast.8) | data formatting | bytes 524288
  99.6 0.0 copy-done.3
  99.6 0.6 copy.26
  100.1 0.0 copy-done.2
  100.1 0.6 copy.27
Async XLA Ops:
  69.9 26.6 %copy-start.1 = (bf16[512,256]{1,0:T(8,128)(2,1)S(1)}, bf16[512,256]{1,0:T(8,128)(2,1)}, u32[]{:S(2)}) copy-start(bf16[512,256]{1,0:T(8,128)(2,1)} %get-tuple-element.22) | copy-start | bytes 786436
  69.9 27.3 %copy-start = (bf16[512,256]{1,0:T(8,128)(2,1)S(1)}, bf16[512,256]{1,0:T(8,128)(2,1)}, u32[]{:S(2)}) copy-start(bf16[512,256]{1,0:T(8,128)(2,1)} %get-tuple-element.23) | copy-start | bytes 786436
  69.9 29.6 %copy-start.3 = (f32[1,256]{1,0:T(1,128)S(1)}, f32[1,256]{1,0:T(1,128)}, u32[]{:S(2)}) copy-start(f32[1,256]{1,0:T(1,128)} %get-tuple-element.27) | copy-start | bytes 3076
  69.9 30.2 %copy-start.2 = (f32[1,256]{1,0:T(1,128)S(1)}, f32[1,256]{1,0:T(1,128)}, u32[]{:S(2)}) copy-start(f32[1,256]{1,0:T(1,128)} %get-tuple-element.28) | copy-start | bytes 3076

commit v2 on v1

v2 whole, which is shorter than its diff:
```python
import functools

import jax
import jax.numpy as jnp
from jax import lax
from jax.experimental import pallas as pl
from jax.experimental.pallas import tpu as pltpu
from jax.sharding import PartitionSpec as P

epsilon = 1e-05
MESH = pl.DeviceIdType.MESH
VM = pl.BlockSpec(memory_space=pltpu.VMEM)
SM = pl.BlockSpec(memory_space=pltpu.SMEM)
ANY = pl.BlockSpec(memory_space=pl.ANY)
f32 = jnp.float32
bf16 = jnp.bfloat16


def place(feat_size, dom_size):
    me_f, me_d = lax.axis_index("feat"), lax.axis_index("dom")
    me = me_f * dom_size + me_d
    total = feat_size * dom_size

    def peer_of(k):
        peer = lax.rem(me + k, total)
        return peer, (lax.div(peer, dom_size), lax.rem(peer, dom_size))

    return me_f, me_d, me, total, peer_of


def meet_all(total, peer_of):
    barrier = pltpu.get_barrier_semaphore()

    def greet(k, carry):
        _, where = peer_of(k)
        pl.semaphore_signal(barrier, inc=1, device_id=where, device_id_type=MESH)
        return carry

    lax.fori_loop(1, total, greet, 0)
    pl.semaphore_wait(barrier, total - 1)


def exchange(me, me_d, total, dom_size, peer_of, source_of, target_of, send_sems, recv_sems):
    def copy(peer, where, landing):
        return pltpu.make_async_remote_copy(
            src_ref=source_of(peer),
            dst_ref=target_of(landing),
            send_sem=send_sems.at[peer],
            recv_sem=recv_sems.at[landing],
            device_id=where,
            device_id_type=MESH,
        )

    def begin_group(group, first):
        def start(k, carry):
            spot = lax.rem(me_d + k, dom_size)
            copy(group * dom_size + spot, (group, spot), me).start()
            return carry

        lax.fori_loop(first, dom_size, start, 0)

    def begin():
        def start(k, carry):
            peer, where = peer_of(k)
            copy(peer, where, me).start()
            return carry

        lax.fori_loop(1, total, start, 0)

    def finish_recv():
        def wait(k, carry):
            peer, where = peer_of(k)
            copy(peer, where, peer).wait_recv()
            return carry

        lax.fori_loop(1, total, wait, 0)

    def finish_send():
        def wait(k, carry):
            peer, where = peer_of(k)
            copy(peer, where, me).wait_send()
            return carry

        lax.fori_loop(1, total, wait, 0)

    return begin, begin_group, finish_recv, finish_send


def selection(rows_ref, count_ref, node_rows):
    rows = rows_ref[0, 0]
    parts, slots = rows.shape
    counts = jnp.broadcast_to(count_ref[0], (slots, parts)).T
    live = lax.broadcasted_iota(jnp.int32, (parts, slots), 1) < counts
    wanted = jnp.where(live, rows, -1)
    nodes = lax.broadcasted_iota(jnp.int32, (parts, slots, node_rows), 2)
    picked = wanted[:, :, None] == nodes
    return jnp.where(picked, 1.0, 0.0).astype(bf16).reshape(parts * slots, node_rows)


def load_turns(vals_ref, vbuf, sems, turns, per_turn):
    def chunk(i):
        span = pl.ds(i * per_turn, per_turn)
        return pltpu.make_async_copy(vals_ref.at[0, 0, span], vbuf.at[span], sems.at[i])

    def start(i, carry):
        chunk(i).start()
        return carry

    lax.fori_loop(0, turns, start, 0)
    return chunk


def dense_kernel(per_turn, from_ref, into_ref, count_ref, vals_ref, hi_ref, lo_ref, scale_ref, acc, vbuf, sems):
    tile = vbuf.shape[1]
    into_blocks = hi_ref.shape[0] // tile
    from_blocks = hi_ref.shape[1] // tile
    spare = into_blocks * from_blocks
    live = count_ref[0, 0]
    turns = lax.div(live + per_turn - 1, per_turn)
    chunk = load_turns(vals_ref, vbuf, sems, turns, per_turn)
    acc[...] = jnp.zeros_like(acc)

    def turn(i, carry):
        chunk(i).wait()
        for j in range(per_turn):
            t = i * per_turn + j
            spot = into_ref[0, 0, t] * from_blocks + from_ref[0, 0, t]
            acc[jnp.where(t < live, spot, spare)] += vbuf[t].astype(f32)
        return carry

    lax.fori_loop(0, turns, turn, 0)
    for b in range(into_blocks):
        span = slice(b * tile, (b + 1) * tile)
        weight = jnp.zeros((tile, tile), f32)
        for s in range(from_blocks):
            value = acc[b * from_blocks + s]
            weight += value
            high = value.astype(bf16)
            hi_ref[span, s * tile:(s + 1) * tile] = high
            lo_ref[span, s * tile:(s + 1) * tile] = (value - high.astype(f32)).astype(bf16)
        inverse = 1.0 / (1.0 + jnp.sum(weight, axis=1, keepdims=True))
        scale_ref[span] = jnp.broadcast_to(inverse, (tile, 128))


def layer_kernel(feat_size, dom_size, tile, x_ref, ws_ref, wn_ref, rows_ref, count_ref, hi_ref, lo_ref,
                 scale_ref, gain_ref, shift_ref, dh_ref,
                 hidden_ref, dself_ref, dneigh_ref, ggrad_ref, sgrad_ref,
                 xbuf, wnbuf, wsbuf, own, summed, neigh, halo, outgoing, pick, pick_t, ah, al, ah_t, al_t,
                 mg, back_out, returned, normed_buf, slope_buf, first, second, local_a, local_b,
                 local_sems, near_send, near_recv, sib_send, sib_recv,
                 send1, recv1, send2, recv2, send3, recv3, send4, recv4):
    me_f, me_d, me, total, peer_of = place(feat_size, dom_size)
    node_rows = x_ref.shape[2]
    columns, width = wn_ref.shape
    slots = rows_ref.shape[3]
    group_rows = dom_size * slots
    halo_rows = total * slots
    nodes = node_rows * total
    half = columns // 2
    side = lax.rem(me_d, 2)
    sibling = me_d + 1 - 2 * side
    mine_rows = pl.ds(pl.multiple_of(side * half, half), half)
    other_rows = pl.ds(pl.multiple_of((1 - side) * half, half), half)
    local_copies = [
        pltpu.make_async_copy(wn_ref, wnbuf.at[me_f], local_sems.at[0]),
        pltpu.make_async_copy(x_ref.at[me_f, 0], xbuf.at[me_f], local_sems.at[1]),
        pltpu.make_async_copy(ws_ref, wsbuf.at[me_f], local_sems.at[2]),
        pltpu.make_async_copy(hi_ref, ah, local_sems.at[3]),
        pltpu.make_async_copy(lo_ref, al, local_sems.at[4]),
    ]
    for copy in local_copies:
        copy.start()
    meet_all(total, peer_of)

    def near(kind, k, arriving):
        other = lax.rem(me_f + k, feat_size)
        landing = other if arriving else me_f
        if kind == 1:
            source, target = x_ref.at[other, 0], xbuf.at[landing]
        else:
            source = (wn_ref, None, ws_ref)[kind].at[mine_rows]
            target = (wnbuf, None, wsbuf)[kind].at[landing, mine_rows]
        return pltpu.make_async_remote_copy(
            src_ref=source,
            dst_ref=target,
            send_sem=near_send.at[kind, other],
            recv_sem=near_recv.at[kind, landing],
            device_id=(other, me_d),
            device_id_type=MESH,
        )

    def passed(kind, k, arriving):
        other = lax.rem(me_f + k, feat_size)
        buffer = (wnbuf, None, wsbuf)[kind]
        return pltpu.make_async_remote_copy(
            src_ref=buffer.at[other, mine_rows],
            dst_ref=buffer.at[other, other_rows if arriving else mine_rows],
            send_sem=sib_send.at[kind, other],
            recv_sem=sib_recv.at[kind, other],
            device_id=(me_f, sibling),
            device_id_type=MESH,
        )

    for kind in range(3):
        for k in range(1, feat_size):
            near(kind, k, False).start()
    pick[...] = selection(rows_ref, count_ref, node_rows)
    for k in range(1, feat_size):
        near(0, k, True).wait_recv()
        passed(0, k, False).start()
    for copy in local_copies:
        copy.wait()

    def turn_block(s, carry):
        lanes = pl.ds(pl.multiple_of(s * tile, tile), tile)
        ah_t[lanes, :] = ah[:, lanes].T
        al_t[lanes, :] = al[:, lanes].T
        return carry

    lax.fori_loop(0, (node_rows + halo_rows) // tile, turn_block, 0)
    summed[...] = jnp.dot(xbuf[me_f], wnbuf[me_f], preferred_element_type=f32)
    for k in range(1, feat_size):
        passed(0, k, True).wait_recv()
        near(1, k, True).wait_recv()
        other = lax.rem(me_f + k, feat_size)
        summed[...] += jnp.dot(xbuf[other], wnbuf[other], preferred_element_type=f32)
    neigh[...] = summed[...].astype(bf16)

    def slots_of(ref):
        return lambda peer: ref.at[pl.ds(pl.multiple_of(peer * slots, slots), slots)]

    mine = pl.ds(pl.multiple_of(me * slots, slots), slots)
    _, begin_group, finish_recv, finish_send1 = exchange(
        me, me_d, total, dom_size, peer_of, slots_of(outgoing), slots_of(halo), send1, recv1)
    for i in range(feat_size):
        group = lax.rem(me_f + i, feat_size)
        span = pl.ds(pl.multiple_of(group * group_rows, group_rows), group_rows)
        outgoing[span] = jnp.dot(pick[span], neigh[...], preferred_element_type=f32).astype(bf16)
        begin_group(group, 1 if i == 0 else 0)
    halo[mine] = outgoing[mine]
    for k in range(1, feat_size):
        near(2, k, True).wait_recv()
        passed(2, k, False).start()
    summed[...] = jnp.dot(ah[:, 0:node_rows], neigh[...], preferred_element_type=f32)
    summed[...] += jnp.dot(al[:, 0:node_rows], neigh[...], preferred_element_type=f32)
    own[...] = jnp.dot(xbuf[me_f], wsbuf[me_f], preferred_element_type=f32)
    for k in range(1, feat_size):
        passed(2, k, True).wait_recv()
        other = lax.rem(me_f + k, feat_size)
        own[...] += jnp.dot(xbuf[other], wsbuf[other], preferred_element_type=f32)

    def turn_pick(s, carry):
        rows = pl.ds(pl.multiple_of(s * tile, tile), tile)
        pick_t[:, rows] = pick[rows, :].T
        return carry

    lax.fori_loop(0, halo_rows // tile, turn_pick, 0)
    finish_recv()
    summed[...] += jnp.dot(ah[:, node_rows:], halo[...], preferred_element_type=f32)
    summed[...] += jnp.dot(al[:, node_rows:], halo[...], preferred_element_type=f32)
    blocks = node_rows // tile
    col_sum = jnp.zeros((1, width), f32)
    col_square = jnp.zeros((1, width), f32)
    for b in range(blocks):
        span = slice(b * tile, (b + 1) * tile)
        pre = own[span] + summed[span] * scale_ref[span, 0:1]
        own[span] = pre
        col_sum += jnp.sum(pre, axis=0, keepdims=True)
        col_square += jnp.sum(pre * pre, axis=0, keepdims=True)
    local_a[0:1] = col_sum
    local_a[1:2] = col_square
    first[me] = local_a[...]
    begin, _, finish_recv, finish_send2 = exchange(
        me, me_d, total, dom_size, peer_of, lambda peer: local_a, lambda peer: first.at[peer], send2, recv2)
    begin()
    finish_recv()
    sums = jnp.sum(first[...], axis=0)
    mean = sums[0:1] / nodes
    variance = sums[1:2] / nodes - mean * mean
    inverse = 1.0 / jnp.sqrt(variance + epsilon)
    gain = gain_ref[...].reshape(1, width)
    shift = shift_ref[...].reshape(1, width)
    slope_sum = jnp.zeros((1, width), f32)
    product_sum = jnp.zeros((1, width), f32)
    for b in range(blocks):
        span = slice(b * tile, (b + 1) * tile)
        normed = (own[span] - mean) * inverse
        act = gain * normed + shift
        logistic = jax.nn.sigmoid(act)
        hidden_ref[span] = (act * logistic).astype(bf16)
        slope = dh_ref[0, 0, span].astype(f32) * logistic * (1.0 + act * (1.0 - logistic))
        normed_buf[span] = normed
        slope_buf[span] = slope
        slope_sum += jnp.sum(slope, axis=0, keepdims=True)
        product_sum += jnp.sum(slope * normed, axis=0, keepdims=True)
    local_b[0:1] = slope_sum
    local_b[1:2] = product_sum
    second[me] = local_b[...]
    begin, _, finish_recv, finish_send3 = exchange(
        me, me_d, total, dom_size, peer_of, lambda peer: local_b, lambda peer: second.at[peer], send3, recv3)
    begin()
    finish_recv()
    sums = jnp.sum(second[...], axis=0)
    shift_grad = sums[0:1] / nodes
    gain_grad = sums[1:2] / nodes
    sgrad_ref[...] = shift_grad
    ggrad_ref[...] = gain_grad
    factor = gain * inverse
    for b in range(blocks):
        span = slice(b * tile, (b + 1) * tile)
        dpre = factor * (slope_buf[span] - shift_grad - normed_buf[span] * gain_grad)
        dself_ref[span] = dpre.astype(bf16)
        mg[span] = (dpre * scale_ref[span, 0:1]).astype(bf16)
    _, begin_group, finish_recv, finish_send4 = exchange(
        me, me_d, total, dom_size, peer_of, slots_of(back_out), slots_of(returned), send4, recv4)
    for i in range(feat_size):
        group = lax.rem(me_f + i, feat_size)
        span = pl.ds(pl.multiple_of(group * group_rows, group_rows), group_rows)
        edges = pl.ds(pl.multiple_of(node_rows + group * group_rows, tile), group_rows)
        back_out[span] = (
            jnp.dot(ah_t[edges], mg[...], preferred_element_type=f32)
            + jnp.dot(al_t[edges], mg[...], preferred_element_type=f32)
        ).astype(bf16)
        begin_group(group, 1 if i == 0 else 0)
    returned[mine] = back_out[mine]
    summed[...] = jnp.dot(ah_t[0:node_rows], mg[...], preferred_element_type=f32)
    summed[...] += jnp.dot(al_t[0:node_rows], mg[...], preferred_element_type=f32)
    for k in range(1, feat_size):
        for kind in range(3):
            near(kind, k, False).wait_send()
        passed(0, k, False).wait_send()
        passed(2, k, False).wait_send()
    finish_send1()
    finish_send2()
    finish_send3()
    finish_recv()
    added = jnp.dot(pick_t[...], returned[...], preferred_element_type=f32)
    dneigh_ref[...] = (summed[...] + added).astype(bf16)
    finish_send4()


def shards(feat_size, dom_size, features, w_self, w_neigh, gain, shift, d_hidden, send_rows, send_count,
           tile_src, tile_dst, tile_count, tile_vals):
    node_rows, columns = features.shape[2], features.shape[3]
    width = w_self.shape[1]
    tiles, tile = tile_vals.shape[2], tile_vals.shape[3]
    parts, slots = send_rows.shape[2], send_rows.shape[3]
    own_blocks = node_rows // tile
    halo_rows = parts * slots
    all_rows = node_rows + halo_rows
    blocks = all_rows // tile
    per_turn = next(n for n in (8, 4, 2, 1) if tiles % n == 0)
    dma = pltpu.SemaphoreType.DMA
    shape = jax.ShapeDtypeStruct
    big = 60 * 1024 * 1024
    high, low, scale = pl.pallas_call(
        functools.partial(dense_kernel, per_turn),
        out_shape=(
            shape((node_rows, all_rows), bf16),
            shape((node_rows, all_rows), bf16),
            shape((node_rows, 128), f32),
        ),
        in_specs=[SM, SM, SM, ANY],
        out_specs=(VM, VM, VM),
        scratch_shapes=[
            pltpu.VMEM((own_blocks * blocks + 1, tile, tile), f32),
            pltpu.VMEM((tiles, tile, tile), bf16),
            dma((tiles // per_turn,)),
        ],
        compiler_params=pltpu.CompilerParams(vmem_limit_bytes=big),
        name="dense",
    )(tile_src, tile_dst, tile_count, tile_vals)
    hidden, d_self, d_neigh, gain_grad, shift_grad = pl.pallas_call(
        functools.partial(layer_kernel, feat_size, dom_size, tile),
        out_shape=(
            shape((node_rows, width), bf16),
            shape((node_rows, width), bf16),
            shape((node_rows, width), bf16),
            shape((1, width), f32),
            shape((1, width), f32),
        ),
        in_specs=[ANY, ANY, ANY, VM, VM, ANY, ANY, VM, VM, VM, VM],
        out_specs=(VM,) * 5,
        scratch_shapes=[
            pltpu.VMEM((feat_size, node_rows, columns), bf16),
            pltpu.VMEM((feat_size, columns, width), bf16),
            pltpu.VMEM((feat_size, columns, width), bf16),
            pltpu.VMEM((node_rows, width), f32),
            pltpu.VMEM((node_rows, width), f32),
            pltpu.VMEM((node_rows, width), bf16),
            pltpu.VMEM((halo_rows, width), bf16),
            pltpu.VMEM((halo_rows, width), bf16),
            pltpu.VMEM((halo_rows, node_rows), bf16),
            pltpu.VMEM((node_rows, halo_rows), bf16),
            pltpu.VMEM((node_rows, all_rows), bf16),
            pltpu.VMEM((node_rows, all_rows), bf16),
            pltpu.VMEM((all_rows, node_rows), bf16),
            pltpu.VMEM((all_rows, node_rows), bf16),
            pltpu.VMEM((node_rows, width), bf16),
            pltpu.VMEM((halo_rows, width), bf16),
            pltpu.VMEM((halo_rows, width), bf16),
            pltpu.VMEM((node_rows, width), f32),
            pltpu.VMEM((node_rows, width), f32),
            pltpu.VMEM((parts, 2, width), f32),
            pltpu.VMEM((parts, 2, width), f32),
            pltpu.VMEM((2, width), f32),
            pltpu.VMEM((2, width), f32),
            dma((5,)), dma((3, feat_size)), dma((3, feat_size)), dma((3, feat_size)), dma((3, feat_size)),
        ] + [dma((parts,)) for _ in range(8)],
        compiler_params=pltpu.CompilerParams(collective_id=0, has_side_effects=True, vmem_limit_bytes=big),
        name="layer",
    )(features, w_self, w_neigh, send_rows, send_count, high, low, scale, gain, shift, d_hidden)
    out_shape = (1, 1, node_rows, width)
    return (
        hidden.reshape(out_shape),
        d_self.reshape(out_shape),
        d_neigh.reshape(out_shape),
        gain_grad.reshape(width),
        shift_grad.reshape(width),
    )


def solution(mesh):
    in_specs = (
        P(None, "dom", None, "feat"),
        P("feat", None),
        P("feat", None),
        P(),
        P(),
        P("feat", "dom", None, None),
        P("feat", "dom", None, None),
        P("feat", "dom", None),
        P("feat", "dom", None),
        P("feat", "dom", None),
        P("feat", "dom"),
        P("feat", "dom", None, None, None),
    )
    out_specs = (
        P("feat", "dom", None, None),
        P("feat", "dom", None, None),
        P("feat", "dom", None, None),
        P(),
        P(),
    )
    body = functools.partial(shards, mesh.shape["feat"], mesh.shape["dom"])
    return jax.shard_map(body, mesh=mesh, in_specs=in_specs, out_specs=out_specs, check_vma=False)
```

time: 102 us -> 81.5 us (0.80)
  Pallas kernels: 95.1 us -> 73.1 us
  local copies, waits for them, and re-layouts: 4.22 us -> 6.14 us
    pallas_call x5 -> x2, Pallas kernels: 95.1 us -> 73.1 us  [the longest x1 68.8 us: shards(): pl.pallas_call(functools.partial(layer_kernel, feat_size, dom_size, tile)...]
    unnamed x13 -> x9, local copies, waits for them, and re-layouts: 4.22 us -> 6.14 us
where the time goes in v2:
time: 81.5 us; the launch traced here: 80.5 us
  Pallas kernels  73.1 us (90%)
  local copies, waits for them, and re-layouts  6.14 us (8%)
  between operations  1.31 us (2%)
    pallas_call x1, Pallas kernels, shards(): pl.pallas_call(functools.partial(layer_kernel, feat_size, dom_size, tile)...  68.8 us
    unnamed x9, local copies, waits for them, and re-layouts  6.14 us
    pallas_call x1, Pallas kernels, shards(): pl.pallas_call(functools.partial(dense_kernel, per_turn), out_shape=(shap...  4.29 us

profile of v2, /device:TPU:0, one launch (start us, length us, event | category | flops | bytes accessed | tf_op | source)
XLA Modules:
  0.0 80.5 jit_solution(5477905358165908748)
XLA Ops:
  1.3 4.3 %dense.1 = (bf16[512,1536]{1,0:T(8,128)(2,1)}, bf16[512,1536]{1,0:T(8,128)(2,1)}, f32[512,128]{1,0:T(8,128)}) custom-call(s32[1,1,136]{2,1,0:T(1,128)} %from_ref.1, s32[1,1,136]{2,1,0:T(1,128)} %into_ref.1, s32[1,1]{1,0:T(1,128)S(6)} %copy.22.count_ref, bf16[1,1,136,128,128]{4,3,2,1,0:T(8,128)(2,1)} %vals_ref.1), custom_call_target="tpu_custom_call" | custom-call | tf_op jit(solution)/shard_map/dense/pallas_call | solution.py:356
  5.6 68.8 %layer.1 = (bf16[512,256]{1,0:T(8,128)(2,1)}, bf16[512,256]{1,0:T(8,128)(2,1)}, bf16[512,256]{1,0:T(8,128)(2,1)}, f32[1,256]{1,0:T(1,128)}, f32[1,256]{1,0:T(1,128)}) custom-call(bf16[4,1,512,256]{3,2,1,0:T(8,128)(2,1)} %x_ref.1, bf16[256,256]{1,0:T(8,128)(2,1)} %ws_ref.1, bf16[256,256]{1,0:T(8,128)(2,1)} %wn_ref.1, s32[1,1,32,32]{3,2,1,0:T(8,128)} %rows_ref.1, ...), custom_call_target="tpu_custom_call" | custom-call | tf_op jit(solution)/shard_map/layer/pallas_call | solution.py:373
  74.3 0.0 copy-start.1
  74.4 0.0 copy-start
  74.4 1.7 %copy.23 = bf16[1,1,512,256]{3,2,1,0:T(8,128)(2,1)} copy(bf16[1,1,512,256]{3,2,1,0:T(8,128)(2,1)} %bitcast.7) | data formatting | bytes 524288
  76.0 1.7 %copy.24 = bf16[1,1,512,256]{3,2,1,0:T(8,128)(2,1)} copy(bf16[1,1,512,256]{3,2,1,0:T(8,128)(2,1)} %bitcast.6) | data formatting | bytes 524288
  77.7 1.7 %copy.25 = bf16[1,1,512,256]{3,2,1,0:T(8,128)(2,1)} copy(bf16[1,1,512,256]{3,2,1,0:T(8,128)(2,1)} %bitcast.5) | data formatting | bytes 524288
  79.4 0.0 copy-done.1
  79.4 0.6 copy.26
  79.9 0.0 copy-done
  79.9 0.6 copy.27
Async XLA Ops:
  74.3 5.0 %copy-start.1 = (f32[1,256]{1,0:T(1,128)S(1)}, f32[1,256]{1,0:T(1,128)}, u32[]{:S(2)}) copy-start(f32[1,256]{1,0:T(1,128)} %get-tuple-element.19) | copy-start | bytes 3076
  74.4 5.6 %copy-start = (f32[1,256]{1,0:T(1,128)S(1)}, f32[1,256]{1,0:T(1,128)}, u32[]{:S(2)}) copy-start(f32[1,256]{1,0:T(1,128)} %get-tuple-element.20) | copy-start | bytes 3076

commit v3 on v2

--- a/solution.py
+++ b/solution.py
@@ -28,7 +28,7 @@
     return me_f, me_d, me, total, peer_of
 
 
-def meet_all(total, peer_of):
+def meet_all(total, peer_of, while_waiting):
     barrier = pltpu.get_barrier_semaphore()
 
     def greet(k, carry):
@@ -37,6 +37,7 @@
         return carry
 
     lax.fori_loop(1, total, greet, 0)
+    while_waiting()
     pl.semaphore_wait(barrier, total - 1)
 
 
@@ -170,7 +171,11 @@
     ]
     for copy in local_copies:
         copy.start()
-    meet_all(total, peer_of)
+
+    def build_pick():
+        pick[...] = selection(rows_ref, count_ref, node_rows)
+
+    meet_all(total, peer_of, build_pick)
 
     def near(kind, k, arriving):
         other = lax.rem(me_f + k, feat_size)
@@ -204,7 +209,6 @@
     for kind in range(3):
         for k in range(1, feat_size):
             near(kind, k, False).start()
-    pick[...] = selection(rows_ref, count_ref, node_rows)
     for k in range(1, feat_size):
         near(0, k, True).wait_recv()
         passed(0, k, False).start()
@@ -339,6 +343,12 @@
     finish_send4()
 
 
+def finish_kernel(*refs):
+    count = len(refs) // 2
+    for source, target in zip(refs[:count], refs[count:]):
+        target[...] = source[...].reshape(target.shape)
+
+
 def shards(feat_size, dom_size, features, w_self, w_neigh, gain, shift, d_hidden, send_rows, send_count,
            tile_src, tile_dst, tile_count, tile_vals):
     node_rows, columns = features.shape[2], features.shape[3]
@@ -411,13 +421,13 @@
         name="layer",
     )(features, w_self, w_neigh, send_rows, send_count, high, low, scale, gain, shift, d_hidden)
     out_shape = (1, 1, node_rows, width)
-    return (
-        hidden.reshape(out_shape),
-        d_self.reshape(out_shape),
-        d_neigh.reshape(out_shape),
-        gain_grad.reshape(width),
-        shift_grad.reshape(width),
-    )
+    return pl.pallas_call(
+        finish_kernel,
+        out_shape=(shape(out_shape, bf16),) * 3 + (shape((width,), f32),) * 2,
+        in_specs=[VM] * 5,
+        out_specs=(VM,) * 5,
+        name="finish",
+    )(hidden, d_self, d_neigh, gain_grad, shift_grad)
 
 
 def solution(mesh):

time: 81.5 us -> 77.1 us (0.946)
  local copies, waits for them, and re-layouts: 6.14 us -> 0 us
  Pallas kernels: 73.1 us -> 74.9 us
    unnamed x9 -> x0, local copies, waits for them, and re-layouts: 6.14 us -> none
    pallas_call x0 -> x1, Pallas kernels: none -> 2.02 us  [shards(): pl.pallas_call(finish_kernel, out_shape=(shape(out_shape, bf16),) * 3 + (...]
    pallas_call x1, Pallas kernels: 68.8 us -> 67.4 us  [shards(): pl.pallas_call(functools.partial(layer_kernel, feat_size, dom_size, tile)...]
    pallas_call x1, Pallas kernels: 4.29 us -> 5.49 us  [shards(): pl.pallas_call(functools.partial(dense_kernel, per_turn), out_shape=(shap...]
where the time goes in v3:
time: 77.1 us; the launch traced here: 76.2 us
  Pallas kernels  74.9 us (97%)
  between operations  1.29 us (2%)
    pallas_call x1, Pallas kernels, shards(): pl.pallas_call(functools.partial(layer_kernel, feat_size, dom_size, tile)...  67.4 us
    pallas_call x1, Pallas kernels, shards(): pl.pallas_call(functools.partial(dense_kernel, per_turn), out_shape=(shap...  5.49 us
    pallas_call x1, Pallas kernels, shards(): pl.pallas_call(finish_kernel, out_shape=(shape(out_shape, bf16),) * 3 + (...  2.02 us

profile of v3, /device:TPU:0, one launch (start us, length us, event | category | flops | bytes accessed | tf_op | source)
XLA Modules:
  0.0 76.2 jit_solution(12951254929115964268)
XLA Ops:
  1.3 5.5 %dense.1 = (bf16[512,1536]{1,0:T(8,128)(2,1)}, bf16[512,1536]{1,0:T(8,128)(2,1)}, f32[512,128]{1,0:T(8,128)}) custom-call(s32[1,1,136]{2,1,0:T(1,128)} %from_ref.1, s32[1,1,136]{2,1,0:T(1,128)} %into_ref.1, s32[1,1]{1,0:T(1,128)S(6)} %copy.17.count_ref, bf16[1,1,136,128,128]{4,3,2,1,0:T(8,128)(2,1)} %vals_ref.1), custom_call_target="tpu_custom_call" | custom-call | tf_op jit(solution)/shard_map/dense/pallas_call | solution.py:366
  6.8 67.4 %layer.1 = (bf16[512,256]{1,0:T(8,128)(2,1)}, bf16[512,256]{1,0:T(8,128)(2,1)}, bf16[512,256]{1,0:T(8,128)(2,1)}, f32[1,256]{1,0:T(1,128)}, f32[1,256]{1,0:T(1,128)}) custom-call(bf16[4,1,512,256]{3,2,1,0:T(8,128)(2,1)} %x_ref.1, bf16[256,256]{1,0:T(8,128)(2,1)} %ws_ref.1, bf16[256,256]{1,0:T(8,128)(2,1)} %wn_ref.1, s32[1,1,32,32]{3,2,1,0:T(8,128)} %rows_ref.1, ...), custom_call_target="tpu_custom_call" | custom-call | tf_op jit(solution)/shard_map/layer/pallas_call | solution.py:383
  74.2 2.0 %finish.1 = (bf16[1,1,512,256]{3,2,1,0:T(8,128)(2,1)}, bf16[1,1,512,256]{3,2,1,0:T(8,128)(2,1)}, bf16[1,1,512,256]{3,2,1,0:T(8,128)(2,1)}, f32[256]{0:T(256)}, f32[256]{0:T(256)}) custom-call(bf16[512,256]{1,0:T(8,128)(2,1)} %get-tuple-element.16.refs_0_, bf16[512,256]{1,0:T(8,128)(2,1)} %get-tuple-element.17.refs_1_, ...), custom_call_target="tpu_custom_call" | custom-call | tf_op jit(solution)/shard_map/finish/pallas_call | solution.py:424

commit v4 on v3

--- a/solution.py
+++ b/solution.py
@@ -98,56 +98,36 @@
     return jnp.where(picked, 1.0, 0.0).astype(bf16).reshape(parts * slots, node_rows)
 
 
-def load_turns(vals_ref, vbuf, sems, turns, per_turn):
-    def chunk(i):
-        span = pl.ds(i * per_turn, per_turn)
-        return pltpu.make_async_copy(vals_ref.at[0, 0, span], vbuf.at[span], sems.at[i])
-
-    def start(i, carry):
-        chunk(i).start()
-        return carry
-
-    lax.fori_loop(0, turns, start, 0)
-    return chunk
-
-
-def dense_kernel(per_turn, from_ref, into_ref, count_ref, vals_ref, hi_ref, lo_ref, scale_ref, acc, vbuf, sems):
-    tile = vbuf.shape[1]
-    into_blocks = hi_ref.shape[0] // tile
-    from_blocks = hi_ref.shape[1] // tile
-    spare = into_blocks * from_blocks
-    live = count_ref[0, 0]
-    turns = lax.div(live + per_turn - 1, per_turn)
-    chunk = load_turns(vals_ref, vbuf, sems, turns, per_turn)
-    acc[...] = jnp.zeros_like(acc)
-
-    def turn(i, carry):
-        chunk(i).wait()
-        for j in range(per_turn):
-            t = i * per_turn + j
-            spot = into_ref[0, 0, t] * from_blocks + from_ref[0, 0, t]
-            acc[jnp.where(t < live, spot, spare)] += vbuf[t].astype(f32)
-        return carry
-
-    lax.fori_loop(0, turns, turn, 0)
-    for b in range(into_blocks):
-        span = slice(b * tile, (b + 1) * tile)
-        weight = jnp.zeros((tile, tile), f32)
-        for s in range(from_blocks):
-            value = acc[b * from_blocks + s]
-            weight += value
-            high = value.astype(bf16)
-            hi_ref[span, s * tile:(s + 1) * tile] = high
-            lo_ref[span, s * tile:(s + 1) * tile] = (value - high.astype(f32)).astype(bf16)
-        inverse = 1.0 / (1.0 + jnp.sum(weight, axis=1, keepdims=True))
-        scale_ref[span] = jnp.broadcast_to(inverse, (tile, 128))
-
-
-def layer_kernel(feat_size, dom_size, tile, x_ref, ws_ref, wn_ref, rows_ref, count_ref, hi_ref, lo_ref,
-                 scale_ref, gain_ref, shift_ref, dh_ref,
+def tile_tables(from_ref, into_ref, live, from_blocks, cells):
+    tiles = from_ref.shape[2]
+    spare = cells
+
+    def turned(row):
+        return jnp.broadcast_to(row, (tiles, tiles)).T
+
+    at = lax.broadcasted_iota(jnp.int32, (1, tiles), 1)
+    key = jnp.where(at < live, into_ref[0] * from_blocks + from_ref[0], spare)
+    key_down = turned(key)
+    down = lax.broadcasted_iota(jnp.int32, (tiles, tiles), 0)
+    across = lax.broadcasted_iota(jnp.int32, (tiles, tiles), 1)
+    before = (key_down < key) | ((key_down == key) & (down < across))
+    rank = jnp.sum(jnp.where(before, 1, 0), axis=0, keepdims=True)
+    lands = turned(rank) == across
+    order = jnp.sum(jnp.where(lands, down, 0), axis=0, keepdims=True)
+    ordered_key = jnp.sum(jnp.where(lands, key_down, 0), axis=0, keepdims=True)
+    cell = lax.broadcasted_iota(jnp.int32, (tiles, cells), 1)
+    key_cells = jnp.broadcast_to(key, (cells, tiles)).T
+    last = jnp.sum(jnp.where(key_cells <= cell, 1, 0), axis=0, keepdims=True) - 1
+    found = jnp.sum(jnp.where(key_cells == cell, 1, 0), axis=0, keepdims=True)
+    return order, ordered_key, last, found
+
+
+def layer_kernel(feat_size, dom_size, tile, x_ref, ws_ref, wn_ref, rows_ref, count_ref, from_ref, into_ref,
+                 live_ref, vals_ref, gain_ref, shift_ref, dh_ref,
                  hidden_ref, dself_ref, dneigh_ref, ggrad_ref, sgrad_ref,
                  xbuf, wnbuf, wsbuf, own, summed, neigh, halo, outgoing, pick, pick_t, ah, al, ah_t, al_t,
                  mg, back_out, returned, normed_buf, slope_buf, first, second, local_a, local_b,
+                 scale_ref, vbuf, history, lists_v, lists_s,
                  local_sems, near_send, near_recv, sib_send, sib_recv,
                  send1, recv1, send2, recv2, send3, recv3, send4, recv4):
     me_f, me_d, me, total, peer_of = place(feat_size, dom_size)
@@ -157,6 +137,10 @@
     group_rows = dom_size * slots
     halo_rows = total * slots
     nodes = node_rows * total
+    tiles = vbuf.shape[0]
+    from_blocks = (node_rows + halo_rows) // tile
+    into_blocks = node_rows // tile
+    cells = into_blocks * from_blocks
     half = columns // 2
     side = lax.rem(me_d, 2)
     sibling = me_d + 1 - 2 * side
@@ -166,14 +150,20 @@
         pltpu.make_async_copy(wn_ref, wnbuf.at[me_f], local_sems.at[0]),
         pltpu.make_async_copy(x_ref.at[me_f, 0], xbuf.at[me_f], local_sems.at[1]),
         pltpu.make_async_copy(ws_ref, wsbuf.at[me_f], local_sems.at[2]),
-        pltpu.make_async_copy(hi_ref, ah, local_sems.at[3]),
-        pltpu.make_async_copy(lo_ref, al, local_sems.at[4]),
+        pltpu.make_async_copy(vals_ref.at[0, 0], vbuf, local_sems.at[3]),
     ]
     for copy in local_copies:
         copy.start()
 
     def build_pick():
         pick[...] = selection(rows_ref, count_ref, node_rows)
+
+        order, ordered_key, last, found = tile_tables(from_ref, into_ref, live_ref[0, 0], from_blocks, cells)
+        lists_v[...] = jnp.zeros_like(lists_v)
+        lists_v[0:1, 0:tiles] = order
+        lists_v[1:2, 0:tiles] = ordered_key
+        lists_v[2:3, 0:cells] = last
+        lists_v[3:4, 0:cells] = found
 
     meet_all(total, peer_of, build_pick)
 
@@ -215,13 +205,36 @@
     for copy in local_copies:
         copy.wait()
 
-    def turn_block(s, carry):
-        lanes = pl.ds(pl.multiple_of(s * tile, tile), tile)
-        ah_t[lanes, :] = ah[:, lanes].T
-        al_t[lanes, :] = al[:, lanes].T
-        return carry
-
-    lax.fori_loop(0, (node_rows + halo_rows) // tile, turn_block, 0)
+    to_scalars = pltpu.make_async_copy(lists_v, lists_s, local_sems.at[4])
+    to_scalars.start()
+    to_scalars.wait()
+
+    def add_tile(r, running):
+        earlier = lists_s[1, jnp.maximum(r - 1, 0)]
+        running = jnp.where(lists_s[1, r] == earlier, running, 0.0) + vbuf[lists_s[0, r]].astype(f32)
+        history[r] = running
+        return running
+
+    lax.fori_loop(0, tiles, add_tile, jnp.zeros((tile, tile), f32), unroll=2)
+    for b in range(into_blocks):
+        span = slice(b * tile, (b + 1) * tile)
+
+        def settle(s, weight):
+            spot = b * from_blocks + s
+            value = history[jnp.maximum(lists_s[2, spot], 0)]
+            value = jnp.where(lists_s[3, spot] > 0, value, 0.0)
+            high = value.astype(bf16)
+            low = (value - high.astype(f32)).astype(bf16)
+            lanes = pl.ds(pl.multiple_of(s * tile, tile), tile)
+            ah[span, lanes] = high
+            al[span, lanes] = low
+            ah_t[lanes, span] = high.T
+            al_t[lanes, span] = low.T
+            return weight + value
+
+        weight = lax.fori_loop(0, from_blocks, settle, jnp.zeros((tile, tile), f32))
+        inverse_degree = 1.0 / (1.0 + jnp.sum(weight, axis=1, keepdims=True))
+        scale_ref[span] = jnp.broadcast_to(inverse_degree, (tile, 128))
     summed[...] = jnp.dot(xbuf[me_f], wnbuf[me_f], preferred_element_type=f32)
     for k in range(1, feat_size):
         passed(0, k, True).wait_recv()
@@ -358,28 +371,11 @@
     own_blocks = node_rows // tile
     halo_rows = parts * slots
     all_rows = node_rows + halo_rows
-    blocks = all_rows // tile
-    per_turn = next(n for n in (8, 4, 2, 1) if tiles % n == 0)
+    cells = own_blocks * (all_rows // tile)
+    list_lanes = -(-max(tiles, cells) // 128) * 128
     dma = pltpu.SemaphoreType.DMA
     shape = jax.ShapeDtypeStruct
     big = 60 * 1024 * 1024
-    high, low, scale = pl.pallas_call(
-        functools.partial(dense_kernel, per_turn),
-        out_shape=(
-            shape((node_rows, all_rows), bf16),
-            shape((node_rows, all_rows), bf16),
-            shape((node_rows, 128), f32),
-        ),
-        in_specs=[SM, SM, SM, ANY],
-        out_specs=(VM, VM, VM),
-        scratch_shapes=[
-            pltpu.VMEM((own_blocks * blocks + 1, tile, tile), f32),
-            pltpu.VMEM((tiles, tile, tile), bf16),
-            dma((tiles // per_turn,)),
-        ],
-        compiler_params=pltpu.CompilerParams(vmem_limit_bytes=big),
-        name="dense",
-    )(tile_src, tile_dst, tile_count, tile_vals)
     hidden, d_self, d_neigh, gain_grad, shift_grad = pl.pallas_call(
         functools.partial(layer_kernel, feat_size, dom_size, tile),
         out_shape=(
@@ -389,7 +385,7 @@
             shape((1, width), f32),
             shape((1, width), f32),
         ),
-        in_specs=[ANY, ANY, ANY, VM, VM, ANY, ANY, VM, VM, VM, VM],
+        in_specs=[ANY, ANY, ANY, VM, VM, VM, VM, SM, ANY, VM, VM, VM],
         out_specs=(VM,) * 5,
         scratch_shapes=[
             pltpu.VMEM((feat_size, node_rows, columns), bf16),
@@ -415,11 +411,16 @@
             pltpu.VMEM((parts, 2, width), f32),
             pltpu.VMEM((2, width), f32),
             pltpu.VMEM((2, width), f32),
+            pltpu.VMEM((node_rows, 128), f32),
+            pltpu.VMEM((tiles, tile, tile), bf16),
+            pltpu.VMEM((tiles, tile, tile), f32),
+            pltpu.VMEM((8, list_lanes), jnp.int32),
+            pltpu.SMEM((8, list_lanes), jnp.int32),
             dma((5,)), dma((3, feat_size)), dma((3, feat_size)), dma((3, feat_size)), dma((3, feat_size)),
         ] + [dma((parts,)) for _ in range(8)],
         compiler_params=pltpu.CompilerParams(collective_id=0, has_side_effects=True, vmem_limit_bytes=big),
         name="layer",
-    )(features, w_self, w_neigh, send_rows, send_count, high, low, scale, gain, shift, d_hidden)
+    )(features, w_self, w_neigh, send_rows, send_count, tile_src, tile_dst, tile_count, tile_vals, gain, shift, d_hidden)
     out_shape = (1, 1, node_rows, width)
     return pl.pallas_call(
         finish_kernel,

time: 77.1 us -> 72.5 us (0.940)
  Pallas kernels: 74.9 us -> 71.1 us
    pallas_call x1 -> x0, Pallas kernels: 5.49 us -> none  [shards(): pl.pallas_call(functools.partial(dense_kernel, per_turn), out_shape=(shap...]
    pallas_call x1, Pallas kernels: 67.4 us -> 69 us  [shards(): pl.pallas_call(functools.partial(layer_kernel, feat_size, dom_size, tile)...]
where the time goes in v4:
time: 72.5 us; the launch traced here: 72.4 us
  Pallas kernels  71.1 us (98%)
  between operations  1.29 us (2%)
    pallas_call x1, Pallas kernels, shards(): pl.pallas_call(functools.partial(layer_kernel, feat_size, dom_size, tile)...  69 us
    pallas_call x1, Pallas kernels, shards(): pl.pallas_call(finish_kernel, out_shape=(shape(out_shape, bf16),) * 3 + (...  2.02 us

profile of v4, /device:TPU:0, one launch (start us, length us, event | category | flops | bytes accessed | tf_op | source)
XLA Modules:
  0.0 72.4 jit_solution(16134492839033336317)
XLA Ops:
  1.3 69.0 %layer.1 = (bf16[512,256]{1,0:T(8,128)(2,1)}, bf16[512,256]{1,0:T(8,128)(2,1)}, bf16[512,256]{1,0:T(8,128)(2,1)}, f32[1,256]{1,0:T(1,128)}, f32[1,256]{1,0:T(1,128)}) custom-call(bf16[4,1,512,256]{3,2,1,0:T(8,128)(2,1)} %x_ref.1, bf16[256,256]{1,0:T(8,128)(2,1)} %ws_ref.1, bf16[256,256]{1,0:T(8,128)(2,1)} %wn_ref.1, s32[1,1,32,32]{3,2,1,0:T(8,128)} %rows_ref.1, ...), custom_call_target="tpu_custom_call" | custom-call | tf_op jit(solution)/shard_map/layer/pallas_call | solution.py:379
  70.3 2.0 %finish.1 = (bf16[1,1,512,256]{3,2,1,0:T(8,128)(2,1)}, bf16[1,1,512,256]{3,2,1,0:T(8,128)(2,1)}, bf16[1,1,512,256]{3,2,1,0:T(8,128)(2,1)}, f32[256]{0:T(256)}, f32[256]{0:T(256)}) custom-call(bf16[512,256]{1,0:T(8,128)(2,1)} %get-tuple-element.10.refs_0_, bf16[512,256]{1,0:T(8,128)(2,1)} %get-tuple-element.11.refs_1_, ...), custom_call_target="tpu_custom_call" | custom-call | tf_op jit(solution)/shard_map/finish/pallas_call | solution.py:425

commit v5 on v4

--- a/solution.py
+++ b/solution.py
@@ -76,6 +76,15 @@
 
         lax.fori_loop(1, total, wait, 0)
 
+    def finish_group(group, first):
+        def wait(k, carry):
+            spot = lax.rem(me_d + k, dom_size)
+            peer = group * dom_size + spot
+            copy(peer, (group, spot), peer).wait_recv()
+            return carry
+
+        lax.fori_loop(first, dom_size, wait, 0)
+
     def finish_send():
         def wait(k, carry):
             peer, where = peer_of(k)
@@ -84,7 +93,7 @@
 
         lax.fori_loop(1, total, wait, 0)
 
-    return begin, begin_group, finish_recv, finish_send
+    return begin, begin_group, finish_recv, finish_group, finish_send
 
 
 def selection(rows_ref, count_ref, node_rows):
@@ -247,7 +256,7 @@
         return lambda peer: ref.at[pl.ds(pl.multiple_of(peer * slots, slots), slots)]
 
     mine = pl.ds(pl.multiple_of(me * slots, slots), slots)
-    _, begin_group, finish_recv, finish_send1 = exchange(
+    _, begin_group, _, finish_group, finish_send1 = exchange(
         me, me_d, total, dom_size, peer_of, slots_of(outgoing), slots_of(halo), send1, recv1)
     for i in range(feat_size):
         group = lax.rem(me_f + i, feat_size)
@@ -272,9 +281,15 @@
         return carry
 
     lax.fori_loop(0, halo_rows // tile, turn_pick, 0)
-    finish_recv()
-    summed[...] += jnp.dot(ah[:, node_rows:], halo[...], preferred_element_type=f32)
-    summed[...] += jnp.dot(al[:, node_rows:], halo[...], preferred_element_type=f32)
+    for i in range(feat_size):
+        group = lax.rem(me_f + feat_size - i, feat_size)
+        span = pl.ds(pl.multiple_of(group * group_rows, group_rows), group_rows)
+        edges = pl.ds(pl.multiple_of(node_rows + group * group_rows, tile), group_rows)
+        finish_group(group, 1 if i == 0 else 0)
+        summed[...] += (
+            jnp.dot(ah[:, edges], halo[span], preferred_element_type=f32)
+            + jnp.dot(al[:, edges], halo[span], preferred_element_type=f32)
+        )
     blocks = node_rows // tile
     col_sum = jnp.zeros((1, width), f32)
     col_square = jnp.zeros((1, width), f32)
@@ -287,7 +302,7 @@
     local_a[0:1] = col_sum
     local_a[1:2] = col_square
     first[me] = local_a[...]
-    begin, _, finish_recv, finish_send2 = exchange(
+    begin, _, finish_recv, _, finish_send2 = exchange(
         me, me_d, total, dom_size, peer_of, lambda peer: local_a, lambda peer: first.at[peer], send2, recv2)
     begin()
     finish_recv()
@@ -313,7 +328,7 @@
     local_b[0:1] = slope_sum
     local_b[1:2] = product_sum
     second[me] = local_b[...]
-    begin, _, finish_recv, finish_send3 = exchange(
+    begin, _, finish_recv, _, finish_send3 = exchange(
         me, me_d, total, dom_size, peer_of, lambda peer: local_b, lambda peer: second.at[peer], send3, recv3)
     begin()
     finish_recv()
@@ -328,7 +343,7 @@
         dpre = factor * (slope_buf[span] - shift_grad - normed_buf[span] * gain_grad)
         dself_ref[span] = dpre.astype(bf16)
         mg[span] = (dpre * scale_ref[span, 0:1]).astype(bf16)
-    _, begin_group, finish_recv, finish_send4 = exchange(
+    _, begin_group, _, finish_group, finish_send4 = exchange(
         me, me_d, total, dom_size, peer_of, slots_of(back_out), slots_of(returned), send4, recv4)
     for i in range(feat_size):
         group = lax.rem(me_f + i, feat_size)
@@ -350,9 +365,15 @@
     finish_send1()
     finish_send2()
     finish_send3()
-    finish_recv()
-    added = jnp.dot(pick_t[...], returned[...], preferred_element_type=f32)
-    dneigh_ref[...] = (summed[...] + added).astype(bf16)
+    for i in range(feat_size):
+        group = lax.rem(me_f + feat_size - i, feat_size)
+        span = pl.ds(pl.multiple_of(group * group_rows, group_rows), group_rows)
+        finish_group(group, 1 if i == 0 else 0)
+        gathered = jnp.dot(pick_t[:, span], returned[span], preferred_element_type=f32)
+        if i < feat_size - 1:
+            summed[...] += gathered
+        else:
+            dneigh_ref[...] = (summed[...] + gathered).astype(bf16)
     finish_send4()
 
 

time: 72.5 us -> 70.9 us (0.978)
  Pallas kernels: 71.1 us -> 69.5 us
    pallas_call x1, Pallas kernels: 69 us -> 67.5 us  [shards(): pl.pallas_call(functools.partial(layer_kernel, feat_size, dom_size, tile)...]
where the time goes in v5:
time: 70.9 us; the launch traced here: 70.8 us
  Pallas kernels  69.5 us (98%)
  between operations  1.29 us (2%)
    pallas_call x1, Pallas kernels, shards(): pl.pallas_call(functools.partial(layer_kernel, feat_size, dom_size, tile)...  67.5 us
    pallas_call x1, Pallas kernels, shards(): pl.pallas_call(finish_kernel, out_shape=(shape(out_shape, bf16),) * 3 + (...  2.02 us

profile of v5, /device:TPU:0, one launch (start us, length us, event | category | flops | bytes accessed | tf_op | source)
XLA Modules:
  0.0 70.8 jit_solution(12022523647042222322)
XLA Ops:
  1.3 67.5 %layer.1 = (bf16[512,256]{1,0:T(8,128)(2,1)}, bf16[512,256]{1,0:T(8,128)(2,1)}, bf16[512,256]{1,0:T(8,128)(2,1)}, f32[1,256]{1,0:T(1,128)}, f32[1,256]{1,0:T(1,128)}) custom-call(bf16[4,1,512,256]{3,2,1,0:T(8,128)(2,1)} %x_ref.1, bf16[256,256]{1,0:T(8,128)(2,1)} %ws_ref.1, bf16[256,256]{1,0:T(8,128)(2,1)} %wn_ref.1, s32[1,1,32,32]{3,2,1,0:T(8,128)} %rows_ref.1, ...), custom_call_target="tpu_custom_call" | custom-call | tf_op jit(solution)/shard_map/layer/pallas_call | solution.py:400
  68.8 2.0 %finish.1 = (bf16[1,1,512,256]{3,2,1,0:T(8,128)(2,1)}, bf16[1,1,512,256]{3,2,1,0:T(8,128)(2,1)}, bf16[1,1,512,256]{3,2,1,0:T(8,128)(2,1)}, f32[256]{0:T(256)}, f32[256]{0:T(256)}) custom-call(bf16[512,256]{1,0:T(8,128)(2,1)} %get-tuple-element.10.refs_0_, bf16[512,256]{1,0:T(8,128)(2,1)} %get-tuple-element.11.refs_1_, ...), custom_call_target="tpu_custom_call" | custom-call | tf_op jit(solution)/shard_map/finish/pallas_call | solution.py:446
